TPU v7x, 512 devices: a whole 4x8x8 slice. The times are simulated.
512 devices in a mesh: lat: 8 (over z), lon: 64 (over y, x, core).
Axes of the slice: x: 4, y: 8, z: 8, core: 2. Of those that a mesh axis runs over, the one named last changes fastest.
Arguments:
- field: bfloat16 [512, 2048, 128], P('lat', 'lon'), may hold values from -6 to 6
- land_mask: int32 [512, 2048], P('lat', 'lon'), may hold values 0 or 1
- zonal_tap_weight: float32 [15, 128], replicated, may hold values from -1.5 to 1.5
- norm_gain: float32 [128], replicated, may hold values from 0.1 to 1.9
- up_weight: bfloat16 [128, 512], replicated, may hold values from -0.5 to 0.5
- down_weight: bfloat16 [512, 128], replicated, may hold values from -0.25 to 0.25
- polar_rows: int32 [256], P('lat'), may hold values from 0 to 63, as said below
- polar_owner: int32 [256], P('lat'), may hold values from 0 to 63, as said below
- polar_taps: float32 [31], replicated, may hold values from -0.8 to 0.8
Outputs:
- mixed_field: bfloat16 [512, 2048, 128], P('lat', 'lon')
- polar_field: bfloat16 [1024, 2048, 128], P(('lat', 'lon'))
Inputs may be any that keep to these rules, and one draw needn't show every extreme that they name: `polar_rows`: within each band the 32 entries are distinct rows in increasing order. `polar_owner`: within each band no owner is named by more than 2 entries, and some owner by exactly 2.
All inputs are finite; a program needn't handle non-finite values. No bound on the sum of `land_mask` on one device may be relied on, other than what follows from the above.
Results may differ from a plain program's by a relative error of at most 0.0059.
Values may be sent and summed in bfloat16 or wider, within the bound.
A program may use at most 64 MiB of HBM per device.

v0:
```python
import jax
import jax.numpy as jnp
from jax import lax
from jax.sharding import PartitionSpec as P

DILATION_STEP = 4


def wrap_pad(block, tap_extent):
    return jnp.concatenate([block[:, -tap_extent:], block, block[:, :tap_extent]], axis=1)


def zonal_branch(padded, stencil_width, zonal_tap_weight, norm_gain, up_weight, down_weight):
    height = padded.shape[0]
    channels = padded.shape[2]
    tap_sum_output = jnp.zeros((height, stencil_width, channels), jnp.float32)
    for zonal_tap_index in range(zonal_tap_weight.shape[0]):
        tap_sum_output = tap_sum_output + zonal_tap_weight[zonal_tap_index] * padded[
            :, zonal_tap_index * DILATION_STEP : zonal_tap_index * DILATION_STEP + stencil_width
        ].astype(jnp.float32)
    average = jnp.mean(tap_sum_output, axis=-1, keepdims=True)
    centred = tap_sum_output - average
    variance = jnp.mean(centred * centred, axis=-1, keepdims=True)
    normed = (centred * lax.rsqrt(variance + 1e-06) * norm_gain).astype(jnp.bfloat16)
    hidden = jax.nn.gelu(
        jnp.dot(normed.reshape(-1, channels), up_weight, preferred_element_type=jnp.float32)
    ).astype(jnp.bfloat16)
    branch = jnp.dot(hidden, down_weight, preferred_element_type=jnp.float32).astype(jnp.bfloat16)
    return branch.reshape(height, stencil_width, channels)


def polar_filter(padded, stencil_width, polar_taps):
    tap_sum_output = jnp.zeros((padded.shape[0], stencil_width, padded.shape[2]), jnp.float32)
    for zonal_tap_index in range(polar_taps.shape[0]):
        tap_sum_output = tap_sum_output + polar_taps[zonal_tap_index] * padded[
            :, zonal_tap_index : zonal_tap_index + stencil_width
        ].astype(jnp.float32)
    return tap_sum_output.astype(jnp.bfloat16)


def body(
    field,
    land_mask,
    zonal_tap_weight,
    norm_gain,
    up_weight,
    down_weight,
    polar_rows,
    polar_owner,
    polar_taps,
):
    lat_rows, lon_cols, channels = field.shape
    lon_tiles = lax.axis_size("lon")
    tap_extent = zonal_tap_weight.shape[0] // 2 * DILATION_STEP
    half_filter = polar_taps.shape[0] // 2
    mask_half = land_mask.astype(jnp.bfloat16)[:, :, None]
    masked = field * mask_half
    strip_rows = lat_rows // lon_tiles
    list_length = polar_rows.shape[0]
    slots_each = max(2, lat_rows // lon_tiles)
    entries = jnp.arange(list_length, dtype=jnp.int32)
    same_owner = (polar_owner[:, None] == polar_owner[None, :]) & (
        entries[None, :] < entries[:, None]
    )
    slot_rank = jnp.sum(same_owner.astype(jnp.int32), axis=1)
    flat_slot = slot_rank * lon_tiles + polar_owner
    slot_ids = jnp.arange(slots_each * lon_tiles, dtype=jnp.int32)
    one_hot = (flat_slot[None, :] == slot_ids[:, None]).astype(jnp.int32)
    occupied = jnp.sum(one_hot, axis=1)
    source_entry = jnp.sum(one_hot * entries[None, :], axis=1)
    valid_half = occupied.astype(jnp.bfloat16)[:, None, None]
    circles = lax.all_to_all(
        masked.reshape(lon_tiles, strip_rows, lon_cols, channels),
        "lon",
        split_axis=0,
        concat_axis=2,
        tiled=True,
    )[0]
    branch_strips = zonal_branch(
        wrap_pad(circles, tap_extent),
        circles.shape[1],
        zonal_tap_weight,
        norm_gain,
        up_weight,
        down_weight,
    )
    branch_tiles = lax.all_to_all(
        branch_strips.reshape(strip_rows, lon_tiles, lon_cols, channels),
        "lon",
        split_axis=1,
        concat_axis=0,
        tiled=True,
    )
    branch_tiles = branch_tiles.reshape(lat_rows, lon_cols, channels)
    mixed_field = (
        (masked.astype(jnp.float32) + branch_tiles.astype(jnp.float32))
        * mask_half.astype(jnp.float32)
    ).astype(jnp.bfloat16)
    outgoing = jnp.take(mixed_field, polar_rows[source_entry], axis=0) * valid_half
    circles = lax.all_to_all(
        outgoing.reshape(slots_each, lon_tiles, lon_cols, channels),
        "lon",
        split_axis=1,
        concat_axis=2,
        tiled=True,
    )[:, 0]
    polar_field = polar_filter(wrap_pad(circles, half_filter), circles.shape[1], polar_taps)
    return (mixed_field, polar_field)


def solution(mesh):
    in_specs = (P("lat", "lon", None), P("lat", "lon"), P(), P(), P(), P(), P("lat"), P("lat"), P())
    out_specs = (P("lat", "lon", None), P(("lat", "lon"), None, None))
    return jax.shard_map(body, mesh=mesh, in_specs=in_specs, out_specs=out_specs, check_vma=False)
```

profile of v0, /device:TPU:1, one launch (start us, length us, event | category | flops | bytes accessed | tf_op | source)
XLA Modules:
  0.0 138.0 jit_solution(6862860365685129678)
XLA Ops:
  0.6 0.0 copy-start
  0.6 0.8 convert_element_type.193
  1.4 0.1 copy.30
  1.5 0.0 copy-start.8
  1.5 0.0 copy-start.5
  1.5 2.2 %multiply_bitcast_fusion = bf16[64,1,32,128]{3,2,1,0:T(8,128)(2,1)} fusion(bf16[64,32,128]{2,1,0:T(8,128)(2,1)} %param.9, bf16[64,32]{1,0:T(8,128)(2,1)S(1)} %copy.30), kind=kLoop, calls=%fused_computation.133 | loop fusion | flops 262144 | bytes 1052672 | tf_op jit(solution)/shard_map/reshape | solution.py:73
  3.7 11.6 %all-to-all-start = ((bf16[64,1,32,128]{3,2,1,0:T(8,128)(2,1)}), bf16[64,1,32,128]{3,2,1,0:T(8,128)(2,1)S(1)}, u32[]{:S(2)}, u32[]{:S(2)}) async-start(bf16[64,1,32,128]{3,2,1,0:T(8,128)(2,1)} %multiply_bitcast_fusion), calls=%async_computation | async-start | bytes 1048576 | tf_op jit(solution)/shard_map/all_to_all | solution.py:72
  15.3 0.0 copy-done.8
  15.3 0.2 convert_reduce_fusion.1
  15.5 0.0 copy-done.5
  15.6 17.5 %all-to-all-done = bf16[64,1,32,128]{3,2,1,0:T(8,128)(2,1)S(1)} async-done(((bf16[64,1,32,128]{3,2,1,0:T(8,128)(2,1)}), bf16[64,1,32,128]{3,2,1,0:T(8,128)(2,1)S(1)}, u32[]{:S(2)}, u32[]{:S(2)}) %all-to-all-start) | async-done | bytes 524320 | tf_op jit(solution)/shard_map/all_to_all | solution.py:72
  33.1 0.0 copy-start.6
  33.1 0.0 copy-start.7
  33.1 8.2 %fusion.67 = (f32[2048]{0:T(1024)S(1)}, f32[1,2048,128]{2,1,0:T(8,128)S(1)}) fusion(bf16[1,28,128]{2,1,0:T(8,128)(2,1)S(1)} %get-tuple-element.9, bf16[1,2048,128]{2,1,0:T(8,128)(2,1)S(1)} %bitcast.92, f32[128]{0:T(128)S(1)} %get-tuple-element.23, f32[128]{0:T(128)S(1)} %get-tuple-element.24, f32[128]{0:T(128)S(1)} %get-tuple-element.11, ...), kind=kLoop, calls=%fused_computation.170 | loop fusion | flops 22804480 | bytes 1603072 | tf_op jit(solution)/shard_map/reduce_sum | solution.py:21
  41.3 0.6 multiply_reduce_fusion
  41.9 0.0 copy-done
  42.0 0.0 copy-done.6
  42.0 0.0 copy-done.7
  42.0 2.7 %convolution_convert_fusion = bf16[2048,128]{1,0:T(8,128)(2,1)} fusion(bf16[512,128]{1,0:T(8,128)(2,1)S(1)} %copy-done, bf16[128,512]{1,0:T(8,128)(2,1)S(1)} %copy-done.6, f32[1,2048,128]{2,1,0:T(8,128)S(1)} %get-tuple-element.5, f32[128]{0:T(128)S(1)} %copy-done.7, f32[2048]{0:T(1024)S(1)} %add_rsqrt_fusion, f32[2048]{0:T(1024)S(1)} %broadcast_multiply_fusion), kind=kOutput, calls=%fused_computation.39 | convolution fusion | flops 547618816 | bytes 1851904 | tf_op jit(solution)/shard_map/dot_general | solution.py:28
  44.7 0.0 copy-start.1
  44.7 0.0 copy-start.3
  44.7 5.9 %all-to-all-start.1 = ((bf16[1,64,32,128]{3,2,0,1:T(8,128)(2,1)}), bf16[1,64,32,128]{3,2,0,1:T(8,128)(2,1)S(1)}, u32[]{:S(2)}, u32[]{:S(2)}) async-start(bf16[1,64,32,128]{3,2,0,1:T(8,128)(2,1)} %bitcast.19), calls=%async_computation.1 | async-start | bytes 1048576 | tf_op jit(solution)/shard_map/all_to_all | solution.py:87
  50.6 0.1 copy.33
  50.7 0.1 convert_reduce_fusion
  50.8 0.0 copy-done.1
  50.8 1.2 gather_fusion
  52.0 0.1 gather.14
  52.1 0.1 copy.34
  52.2 0.1 convert_element_type.220
  52.3 0.1 copy.36
  52.4 15.8 %all-to-all-done.1 = bf16[1,64,32,128]{3,2,0,1:T(8,128)(2,1)S(1)} async-done(((bf16[1,64,32,128]{3,2,0,1:T(8,128)(2,1)}), bf16[1,64,32,128]{3,2,0,1:T(8,128)(2,1)S(1)}, u32[]{:S(2)}, u32[]{:S(2)}) %all-to-all-start.1) | async-done | bytes 524320 | tf_op jit(solution)/shard_map/all_to_all | solution.py:87
  68.3 0.0 copy-done.3
  68.3 0.6 fusion.37
  68.9 0.0 copy-start.2
  68.9 0.8 gather_fusion.1
  69.7 0.0 copy-done.2
  69.7 1.3 fusion.38
  71.0 0.0 copy-start.4
  71.0 5.9 %all-to-all-start.2 = ((bf16[2,64,32,128]{3,2,0,1:T(8,128)(2,1)}), bf16[2,64,32,128]{3,2,0,1:T(8,128)(2,1)S(1)}, u32[]{:S(2)}, u32[]{:S(2)}) async-start(bf16[2,64,32,128]{3,2,0,1:T(8,128)(2,1)} %fusion.38), calls=%async_computation.2 | async-start | bytes 2097152 | tf_op jit(solution)/shard_map/all_to_all | solution.py:100
  76.8 0.0 copy-done.4
  76.9 0.7 fusion.71
  77.6 0.7 fusion.70
  78.3 26.5 %all-to-all-done.2 = bf16[2,64,32,128]{3,2,0,1:T(8,128)(2,1)S(1)} async-done(((bf16[2,64,32,128]{3,2,0,1:T(8,128)(2,1)}), bf16[2,64,32,128]{3,2,0,1:T(8,128)(2,1)S(1)}, u32[]{:S(2)}, u32[]{:S(2)}) %all-to-all-start.2) | async-done | bytes 1048608 | tf_op jit(solution)/shard_map/all_to_all | solution.py:100
  104.8 0.1 copy.37
  104.9 33.1 %add_convert_fusion = bf16[2,2048,128]{2,1,0:T(8,128)(2,1)} fusion(bf16[2,2048,128]{2,1,0:T(8,128)(2,1)S(1)} %bitcast.89, bf16[2,15,128]{2,1,0:T(8,128)(2,1)S(1)} %get-tuple-element.7, bf16[2,15,128]{2,1,0:T(8,128)(2,1)S(1)} %get-tuple-element.6, f32[]{:T(128)} %bitcast.58, f32[]{:T(128)} %bitcast.57, f32[]{:T(128)} %bitcast.56, f32[]{:T(128)} %bitcast.55, ...), kind=kLoop, calls=%fused_computation.40 | loop fusion | flops 95944704 | bytes 2112636 | tf_op jit(solution)/shard_map/convert_element_type | solution.py:38
  (12 shorter events, 0.1 us)
Async XLA Ops:
  0.6 41.3 %copy-start = (bf16[512,128]{1,0:T(8,128)(2,1)S(1)}, bf16[512,128]{1,0:T(8,128)(2,1)}, u32[]{:S(2)}) copy-start(bf16[512,128]{1,0:T(8,128)(2,1)} %param.14) | copy-start | bytes 393220
  1.5 13.8 %copy-start.8 = (s32[32]{0:T(128)S(1)}, s32[32]{0:T(128)}, u32[]{:S(2)}) copy-start(s32[32]{0:T(128)} %param.16) | copy-start | bytes 388
  1.5 14.0 %copy-start.5 = (f32[15,128]{1,0:T(8,128)S(1)}, f32[15,128]{1,0:T(8,128)}, u32[]{:S(2)}) copy-start(f32[15,128]{1,0:T(8,128)} %param.11) | copy-start | bytes 23044
  3.7 29.3 %all-to-all-start = ((bf16[64,1,32,128]{3,2,1,0:T(8,128)(2,1)}), bf16[64,1,32,128]{3,2,1,0:T(8,128)(2,1)S(1)}, u32[]{:S(2)}, u32[]{:S(2)}) async-start(bf16[64,1,32,128]{3,2,1,0:T(8,128)(2,1)} %multiply_bitcast_fusion), calls=%async_computation | async-start | bytes 1048576 | tf_op jit(solution)/shard_map/all_to_all | solution.py:72
  33.1 8.9 %copy-start.6 = (bf16[128,512]{1,0:T(8,128)(2,1)S(1)}, bf16[128,512]{1,0:T(8,128)(2,1)}, u32[]{:S(2)}) copy-start(bf16[128,512]{1,0:T(8,128)(2,1)} %param.13) | copy-start | bytes 393220
  33.1 8.9 %copy-start.7 = (f32[128]{0:T(128)S(1)}, f32[128]{0:T(128)}, u32[]{:S(2)}) copy-start(f32[128]{0:T(128)} %param.12) | copy-start | bytes 1540
  44.7 6.1 %copy-start.1 = (s32[32]{0:T(128)S(1)}, s32[32]{0:T(128)}, u32[]{:S(2)}) copy-start(s32[32]{0:T(128)} %param.15) | copy-start | bytes 388
  44.7 23.6 %copy-start.3 = (bf16[64,32,128]{2,1,0:T(8,128)(2,1)S(1)}, bf16[64,32,128]{2,1,0:T(8,128)(2,1)}, u32[]{:S(2)}) copy-start(bf16[64,32,128]{2,1,0:T(8,128)(2,1)} %param.9) | copy-start | bytes 1572868
  44.7 23.6 %all-to-all-start.1 = ((bf16[1,64,32,128]{3,2,0,1:T(8,128)(2,1)}), bf16[1,64,32,128]{3,2,0,1:T(8,128)(2,1)S(1)}, u32[]{:S(2)}, u32[]{:S(2)}) async-start(bf16[1,64,32,128]{3,2,0,1:T(8,128)(2,1)} %bitcast.19), calls=%async_computation.1 | async-start | bytes 1048576 | tf_op jit(solution)/shard_map/all_to_all | solution.py:87
  68.9 0.8 copy-start.2
  71.0 5.9 %copy-start.4 = (f32[31]{0:T(128)S(1)}, f32[31]{0:T(128)}, u32[]{:S(2)}) copy-start(f32[31]{0:T(128)} %param.17) | copy-start | bytes 376
  71.0 33.8 %all-to-all-start.2 = ((bf16[2,64,32,128]{3,2,0,1:T(8,128)(2,1)}), bf16[2,64,32,128]{3,2,0,1:T(8,128)(2,1)S(1)}, u32[]{:S(2)}, u32[]{:S(2)}) async-start(bf16[2,64,32,128]{3,2,0,1:T(8,128)(2,1)} %fusion.38), calls=%async_computation.2 | async-start | bytes 2097152 | tf_op jit(solution)/shard_map/all_to_all | solution.py:100
where the time goes:
time: 139 us; the launch traced here: 138 us
  waiting for transfers between devices  59.9 us (43%)
  other arithmetic  47.1 us (34%)
  starting transfers between devices  23.3 us (17%)
  local copies, waits for them, and re-layouts  4.16 us (3%)
  matrix products  2.71 us (2%)
    convert_element_type x1, other arithmetic, polar_filter(): return tap_sum_output.astype(jnp.bfloat16)  33.1 us
    all_to_all x1, waiting for transfers between devices, body(): lax.all_to_all(outgoing.reshape(slots_each, lon_tiles, lon_cols, channels...  26.5 us
    all_to_all x1, waiting for transfers between devices, body(): lax.all_to_all(masked.reshape(lon_tiles, strip_rows, lon_cols, channels),...  17.5 us
    all_to_all x1, waiting for transfers between devices, body(): lax.all_to_all(branch_strips.reshape(strip_rows, lon_tiles, lon_cols, cha...  15.8 us
    all_to_all x1, starting transfers between devices, body(): lax.all_to_all(masked.reshape(lon_tiles, strip_rows, lon_cols, channels),...  11.6 us
    reduce_sum x1, other arithmetic, zonal_branch(): average = jnp.mean(tap_sum_output, axis=-1, keepdims=True)  8.2 us
    all_to_all x1, starting transfers between devices, body(): lax.all_to_all(branch_strips.reshape(strip_rows, lon_tiles, lon_cols, cha...  5.86 us
    all_to_all x1, starting transfers between devices, body(): lax.all_to_all(outgoing.reshape(slots_each, lon_tiles, lon_cols, channels...  5.85 us
  transfers between devices with their start and end apart: 3, of which 3 were waited for; matrix products, arithmetic and copies ran while one was open for 3% of the time, Pallas kernels for 0%

commit v1 on v0

v1 whole, which is shorter than its diff:
```python
import functools

import jax
import jax.numpy as jnp
from jax import lax
from jax.experimental import pallas as pl
from jax.experimental.pallas import tpu as pltpu
from jax.sharding import PartitionSpec as P

DILATION = 4
LAND = 64.0
GELU_A = 0.7978845608028654
GELU_B = 0.044715 * GELU_A


def vmem():
    return pl.BlockSpec(memory_space=pltpu.VMEM)


def smem():
    return pl.BlockSpec(memory_space=pltpu.SMEM)


def mix(tiles, keep, taps, gain, up, down):
    rows = tiles.shape[0]
    channels = tiles.shape[-1]
    land = tiles == LAND
    tiles = jnp.where(land, 0.0, tiles)
    turned = pltpu.roll(tiles.reshape(rows * (keep + 8), 8, channels), 4, 1).reshape(tiles.shape)
    first_half = lax.broadcasted_iota(jnp.int32, (rows, keep + 7, 8, channels), 2) < 4
    halves = jnp.where(first_half, turned[:, :-1], turned[:, 1:])
    zonal = None
    for k in range(taps.shape[0]):
        start = (k - 7) * DILATION + 32
        source = halves if start % 8 else tiles
        term = taps[k][None, None, None, :] * source[:, start // 8 : start // 8 + keep]
        zonal = term if zonal is None else zonal + term
    zonal = zonal.reshape(rows * keep * 8, channels)
    centred = zonal - jnp.mean(zonal, axis=-1, keepdims=True)
    variance = jnp.mean(centred * centred, axis=-1, keepdims=True)
    normed = (centred * lax.rsqrt(variance + 1e-06) * gain).astype(jnp.bfloat16)
    hidden = jnp.dot(normed, up, preferred_element_type=jnp.float32)
    bent = jnp.tanh(hidden * (GELU_A + GELU_B * (hidden * hidden)))
    half = 0.5 * hidden
    hidden = (half + half * bent).astype(jnp.bfloat16)
    branch = jnp.dot(hidden, down, preferred_element_type=jnp.float32).astype(jnp.bfloat16)
    centre = slice(4, 4 + keep)
    mixed = tiles[:, centre].reshape(-1, channels) + branch.astype(jnp.float32)
    return jnp.where(land[:, centre].reshape(-1, channels), 0.0, mixed).astype(jnp.bfloat16)


def prepare_kernel(rows_ref, owner_ref, field_ref, mask_ref, coded_ref, send_ref, table):
    lat_rows, cols, channels = field_ref.shape
    owners = send_ref.shape[0]
    for r in range(0, lat_rows, 8):
        wet = mask_ref[r : r + 8][:, :, None]
        coded_ref[r : r + 8] = jnp.where(
            jnp.broadcast_to(wet, (8, cols, channels)) != 0,
            field_ref[r : r + 8].astype(jnp.float32),
            LAND,
        ).astype(jnp.bfloat16)
    send_ref[...] = jnp.full_like(send_ref, LAND)

    @pl.loop(0, owners)
    def _(o):
        table[o] = 0

    @pl.loop(0, rows_ref.shape[0])
    def _(e):
        owner = owner_ref[e]
        rank = table[owner]
        table[owner] = rank + 1
        send_ref[owner, rank] = coded_ref[rows_ref[e]]


def prepare(field, land_mask, polar_rows, polar_owner, owners, slots):
    lat_rows, cols, channels = field.shape
    return pl.pallas_call(
        prepare_kernel,
        out_shape=(
            jax.ShapeDtypeStruct(field.shape, jnp.bfloat16),
            jax.ShapeDtypeStruct((owners, slots, cols, channels), jnp.bfloat16),
        ),
        in_specs=[smem(), smem(), vmem(), vmem()],
        out_specs=(vmem(), vmem()),
        scratch_shapes=[pltpu.SMEM((owners,), jnp.int32)],
    )(polar_rows, polar_owner, field, land_mask)


def own_kernel(left_ref, own_ref, right_ref, taps_ref, gain_ref, up_ref, down_ref, out_ref):
    lat_rows, cols, channels = own_ref.shape
    step = 8

    @pl.loop(0, lat_rows // step)
    def _(i):
        rows = pl.ds(i * step, step)
        tiles = jnp.concatenate(
            [
                ref[rows].astype(jnp.float32).reshape(step, cols // 8, 8, channels)
                for ref in (left_ref, own_ref, right_ref)
            ],
            axis=1,
        )
        mixed = mix(tiles, cols // 8, taps_ref, gain_ref[...], up_ref[...], down_ref[...])
        out_ref[rows] = mixed.reshape(step, cols, channels)


def own(left, coded, right, taps, gain, up, down):
    return pl.pallas_call(
        own_kernel,
        out_shape=jax.ShapeDtypeStruct(coded.shape, jnp.bfloat16),
        in_specs=[vmem()] * 7,
        out_specs=vmem(),
    )(left, coded, right, taps, gain, up, down)


def polar_kernel(raw_ref, taps_ref, gain_ref, up_ref, down_ref, line_ref, out_ref, padded, mixed):
    tiles, slots, cols, channels = raw_ref.shape
    length = tiles * cols
    chunk = 256
    block = 128
    wide = block + 2 * cols
    band = pltpu.roll(jnp.broadcast_to(line_ref[...], (block, 256)), 0, 1, stride=1, stride_axis=0)
    band = band[:, :wide]
    high = band.astype(jnp.bfloat16)
    low = (band - high.astype(jnp.float32)).astype(jnp.bfloat16)
    for s in range(slots):
        padded[0:cols] = raw_ref[tiles - 1, s]
        padded[cols + length : length + 2 * cols] = raw_ref[0, s]
        padded[cols : cols + length] = raw_ref[:, s].reshape(length, channels)

        @pl.loop(0, length // chunk)
        def _(i):
            at = pl.multiple_of(i * chunk, chunk)
            tile = padded[pl.ds(at, chunk + 2 * cols)].astype(jnp.float32)
            tile = tile.reshape(1, (chunk + 2 * cols) // 8, 8, channels)
            mixed[pl.ds(cols + at, chunk)] = mix(
                tile, chunk // 8, taps_ref, gain_ref[...], up_ref[...], down_ref[...]
            )

        mixed[0:cols] = mixed[length : length + cols]
        mixed[cols + length : length + 2 * cols] = mixed[cols : 2 * cols]

        @pl.loop(0, length // block)
        def _(i):
            at = pl.multiple_of(i * block, block)
            window = mixed[pl.ds(at, wide)]
            total = jnp.dot(high, window, preferred_element_type=jnp.float32)
            total += jnp.dot(low, window, preferred_element_type=jnp.float32)
            out_ref[s, pl.ds(at, block)] = total.astype(jnp.bfloat16)


def polar(raw, taps, gain, up, down, line):
    tiles, slots, cols, channels = raw.shape
    length = tiles * cols
    return pl.pallas_call(
        polar_kernel,
        out_shape=jax.ShapeDtypeStruct((slots, length, channels), jnp.bfloat16),
        in_specs=[vmem()] * 6,
        out_specs=vmem(),
        scratch_shapes=[
            pltpu.VMEM((length + 2 * cols, channels), jnp.bfloat16),
            pltpu.VMEM((length + 2 * cols, channels), jnp.bfloat16),
        ],
    )(raw, taps, gain, up, down, line)


def body(field, land_mask, taps, gain, up, down, polar_rows, polar_owner, polar_taps):
    owners = lax.axis_size("lon")
    slots = 2
    gain = gain[None, :]
    coded, outgoing = prepare(field, land_mask, polar_rows, polar_owner, owners, slots)
    raw = lax.all_to_all(outgoing, "lon", split_axis=0, concat_axis=0, tiled=True)
    ahead = [(i, (i + 1) % owners) for i in range(owners)]
    back = [(i, (i - 1) % owners) for i in range(owners)]
    left = lax.ppermute(coded, "lon", ahead)
    right = lax.ppermute(coded, "lon", back)
    mixed_field = own(left, coded, right, taps, gain, up, down)
    cols = field.shape[1]
    half = polar_taps.shape[0] // 2
    line = jnp.zeros((1, 256), jnp.float32)
    line = lax.dynamic_update_slice(line, polar_taps[None, :], (0, cols - half))
    polar_field = polar(raw, taps, gain, up, down, line)
    return (mixed_field, polar_field)


def solution(mesh):
    in_specs = (P("lat", "lon", None), P("lat", "lon"), P(), P(), P(), P(), P("lat"), P("lat"), P())
    out_specs = (P("lat", "lon", None), P(("lat", "lon"), None, None))
    return jax.shard_map(body, mesh=mesh, in_specs=in_specs, out_specs=out_specs, check_vma=False)
```

time: 139 us -> 78.3 us (0.56)
  the two profiles are of different devices: /device:TPU:1 before, /device:TPU:448 now
where the time goes in v1:
time: 78.3 us; the launch traced here: 77.9 us
  Pallas kernels  29.3 us (37%)
  waiting for transfers between devices  24.6 us (31%)
  starting transfers between devices  19.5 us (25%)
  local copies, waits for them, and re-layouts  3.84 us (5%)
    ppermute x1, waiting for transfers between devices, body(): right = lax.ppermute(coded, 'lon', back)  19 us
    pallas_call x1, Pallas kernels, polar(): pl.pallas_call(polar_kernel, out_shape=jax.ShapeDtypeStruct((slots, lengt...  18.4 us
    all_to_all x1, starting transfers between devices, body(): lax.all_to_all(outgoing, 'lon', split_axis=0, concat_axis=0, tiled=True)  10.7 us
    pallas_call x1, Pallas kernels, own(): pl.pallas_call(own_kernel, out_shape=jax.ShapeDtypeStruct(coded.shape, jn...  7.6 us
    ppermute x1, starting transfers between devices, body(): right = lax.ppermute(coded, 'lon', back)  6.86 us
    ppermute x1, waiting for transfers between devices, body(): left = lax.ppermute(coded, 'lon', ahead)  5.62 us
    pallas_call x1, Pallas kernels, prepare(): pl.pallas_call(prepare_kernel, out_shape=(jax.ShapeDtypeStruct(field.shap...  3.34 us
    unnamed x11, local copies, waits for them, and re-layouts  3.17 us
  transfers between devices with their start and end apart: 3, of which 2 were waited for; matrix products, arithmetic and copies ran while one was open for 1% of the time, Pallas kernels for 10%

profile of v1, /device:TPU:448, one launch (start us, length us, event | category | flops | bytes accessed | tf_op | source)
XLA Modules:
  0.0 77.9 jit_solution(7983259859828084481)
XLA Ops:
  0.6 1.4 %copy.11.mask_ref = s32[64,32]{1,0:T(8,128)} copy(s32[64,32]{0,1:T(8,128)} %param.10) | data formatting | bytes 16384 | tf_op args[1]
  2.0 3.3 %shard_map.104 = (bf16[64,32,128]{2,1,0:T(8,128)(2,1)}, bf16[64,2,32,128]{3,2,1,0:T(8,128)(2,1)}) custom-call(s32[32]{0:T(128)} %rows_ref.1, s32[32]{0:T(128)} %owner_ref.1, bf16[64,32,128]{2,1,0:T(8,128)(2,1)} %field_ref.1, s32[64,32]{1,0:T(8,128)} %copy.11.mask_ref), custom_call_target="tpu_custom_call" | custom-call | tf_op jit(solution)/shard_map/pallas_call | solution.py:78
  5.4 0.0 copy-start.1
  5.4 10.7 %all-to-all-start = ((bf16[64,2,32,128]{3,2,1,0:T(8,128)(2,1)}), bf16[64,2,32,128]{3,2,1,0:T(8,128)(2,1)S(1)}, u32[]{:S(2)}, u32[]{:S(2)}) async-start(bf16[64,2,32,128]{3,2,1,0:T(8,128)(2,1)} %get-tuple-element.5), calls=%async_computation | async-start | bytes 2097152 | tf_op jit(solution)/shard_map/all_to_all | solution.py:173
  16.1 0.0 copy-done.1
  16.1 0.0 copy-start.4
  16.1 6.9 %collective-permute-start.1 = (bf16[64,32,128]{2,1,0:T(8,128)(2,1)S(1)}, bf16[64,32,128]{2,1,0:T(8,128)(2,1)S(1)}, u32[]{:S(2)}, u32[]{:S(2)}) collective-permute-start(bf16[64,32,128]{2,1,0:T(8,128)(2,1)S(1)} %copy-done.1), channel_id=1, source_target_pairs={{0,63},{1,0},{2,1},{3,2},{4,3},{5,4},{6,5},{7,6},{8,7},{9,8},{10,9... | collective-permute-start | bytes 1572872 | tf_op jit(solution)/shard_map/ppermute | solution.py:177
  23.0 1.9 %collective-permute-start = (bf16[64,32,128]{2,1,0:T(8,128)(2,1)S(1)}, bf16[64,32,128]{2,1,0:T(8,128)(2,1)S(1)}, u32[]{:S(2)}, u32[]{:S(2)}) collective-permute-start(bf16[64,32,128]{2,1,0:T(8,128)(2,1)S(1)} %copy-done.1), channel_id=1, source_target_pairs={{0,1},{1,2},{2,3},{3,4},{4,5},{5,6},{6,7},{7,8},{8,9},{9,10},{10,1... | collective-permute-start | bytes 1572872 | tf_op jit(solution)/shard_map/ppermute | solution.py:176
  24.9 0.0 copy-done.4
  24.9 0.7 dynamic_update_slice.3.line_ref
  25.6 19.0 %collective-permute-done.1.right_ref = bf16[64,32,128]{2,1,0:T(8,128)(2,1)S(1)} collective-permute-done((bf16[64,32,128]{2,1,0:T(8,128)(2,1)S(1)}, bf16[64,32,128]{2,1,0:T(8,128)(2,1)S(1)}, u32[]{:S(2)}, u32[]{:S(2)}) %collective-permute-start.1) | collective-permute-done | bytes 524320 | tf_op jit(solution)/shard_map/ppermute | solution.py:177
  44.6 0.0 copy-start.2
  44.6 5.6 %collective-permute-done.left_ref = bf16[64,32,128]{2,1,0:T(8,128)(2,1)S(1)} collective-permute-done((bf16[64,32,128]{2,1,0:T(8,128)(2,1)S(1)}, bf16[64,32,128]{2,1,0:T(8,128)(2,1)S(1)}, u32[]{:S(2)}, u32[]{:S(2)}) %collective-permute-start) | collective-permute-done | bytes 524320 | tf_op jit(solution)/shard_map/ppermute | solution.py:176
  50.2 0.0 copy-start.3
  50.2 0.0 copy-done.2
  50.2 0.8 copy-done.3
  51.0 7.6 %shard_map.105 = bf16[64,32,128]{2,1,0:T(8,128)(2,1)} custom-call(bf16[64,32,128]{2,1,0:T(8,128)(2,1)} %copy-done.3, bf16[64,32,128]{2,1,0:T(8,128)(2,1)} %get-tuple-element.4.own_ref, bf16[64,32,128]{2,1,0:T(8,128)(2,1)} %copy-done.2, f32[15,128]{1,0:T(8,128)} %taps_ref.3, f32[1,128]{1,0:T(1,128)} %bitcast.2, bf16[128,512]{1,0:T(8,128)(2,1)} %up_ref.3, ...), custom_call_target="tpu_custom_call" | custom-call | tf_op jit(solution)/shard_map/pallas_call | solution.py:109
  58.6 0.0 all-to-all-done.raw_ref
  58.6 0.0 copy-start
  58.6 1.0 %copy-done = bf16[64,2,32,128]{3,2,1,0:T(8,128)(2,1)} copy-done((bf16[64,2,32,128]{3,2,1,0:T(8,128)(2,1)}, bf16[64,2,32,128]{3,2,1,0:T(8,128)(2,1)S(1)}, u32[]{:S(2)}) %copy-start) | copy-done | bytes 1048600
  59.6 18.4 %shard_map.106 = bf16[2,2048,128]{2,1,0:T(8,128)(2,1)} custom-call(bf16[64,2,32,128]{3,2,1,0:T(8,128)(2,1)} %copy-done, f32[15,128]{1,0:T(8,128)} %taps_ref.3, f32[1,128]{1,0:T(1,128)} %bitcast.3, bf16[128,512]{1,0:T(8,128)(2,1)} %up_ref.3, bf16[512,128]{1,0:T(8,128)(2,1)} %down_ref.3, f32[1,256]{1,0:T(1,128)} %dynamic_update_slice.3.line_ref), custom_call_target="tpu_custom_call" | custom-call | tf_op jit(solution)/shard_map/pallas_call | solution.py:156
Async XLA Ops:
  5.4 10.7 %copy-start.1 = (bf16[64,32,128]{2,1,0:T(8,128)(2,1)S(1)}, bf16[64,32,128]{2,1,0:T(8,128)(2,1)}, u32[]{:S(2)}) copy-start(bf16[64,32,128]{2,1,0:T(8,128)(2,1)} %get-tuple-element.4.own_ref) | copy-start | bytes 1572868
  5.4 53.2 %all-to-all-start = ((bf16[64,2,32,128]{3,2,1,0:T(8,128)(2,1)}), bf16[64,2,32,128]{3,2,1,0:T(8,128)(2,1)S(1)}, u32[]{:S(2)}, u32[]{:S(2)}) async-start(bf16[64,2,32,128]{3,2,1,0:T(8,128)(2,1)} %get-tuple-element.5), calls=%async_computation | async-start | bytes 2097152 | tf_op jit(solution)/shard_map/all_to_all | solution.py:173
  16.1 8.8 %copy-start.4 = (f32[31]{0:T(128)S(1)}, f32[31]{0:T(128)}, u32[]{:S(2)}) copy-start(f32[31]{0:T(128)} %param.17) | copy-start | bytes 376
  16.1 28.5 %collective-permute-start.1 = (bf16[64,32,128]{2,1,0:T(8,128)(2,1)S(1)}, bf16[64,32,128]{2,1,0:T(8,128)(2,1)S(1)}, u32[]{:S(2)}, u32[]{:S(2)}) collective-permute-start(bf16[64,32,128]{2,1,0:T(8,128)(2,1)S(1)} %copy-done.1), channel_id=1, source_target_pairs={{0,63},{1,0},{2,1},{3,2},{4,3},{5,4},{6,5},{7,6},{8,7},{9,8},{10,9... | collective-permute-start | bytes 1572872 | tf_op jit(solution)/shard_map/ppermute | solution.py:177
  23.0 27.2 %collective-permute-start = (bf16[64,32,128]{2,1,0:T(8,128)(2,1)S(1)}, bf16[64,32,128]{2,1,0:T(8,128)(2,1)S(1)}, u32[]{:S(2)}, u32[]{:S(2)}) collective-permute-start(bf16[64,32,128]{2,1,0:T(8,128)(2,1)S(1)} %copy-done.1), channel_id=1, source_target_pairs={{0,1},{1,2},{2,3},{3,4},{4,5},{5,6},{6,7},{7,8},{8,9},{9,10},{10,1... | collective-permute-start | bytes 1572872 | tf_op jit(solution)/shard_map/ppermute | solution.py:176
  44.6 5.6 %copy-start.2 = (bf16[64,32,128]{2,1,0:T(8,128)(2,1)}, bf16[64,32,128]{2,1,0:T(8,128)(2,1)S(1)}, u32[]{:S(2)}) copy-start(bf16[64,32,128]{2,1,0:T(8,128)(2,1)S(1)} %collective-permute-done.1.right_ref) | copy-start | bytes 1572868
  50.2 0.8 %copy-start.3 = (bf16[64,32,128]{2,1,0:T(8,128)(2,1)}, bf16[64,32,128]{2,1,0:T(8,128)(2,1)S(1)}, u32[]{:S(2)}) copy-start(bf16[64,32,128]{2,1,0:T(8,128)(2,1)S(1)} %collective-permute-done.left_ref) | copy-start | bytes 1572868
  58.6 1.0 %copy-start = (bf16[64,2,32,128]{3,2,1,0:T(8,128)(2,1)}, bf16[64,2,32,128]{3,2,1,0:T(8,128)(2,1)S(1)}, u32[]{:S(2)}) copy-start(bf16[64,2,32,128]{3,2,1,0:T(8,128)(2,1)S(1)} %all-to-all-done.raw_ref) | copy-start | bytes 3145732

commit v2 on v1

--- a/solution.py
+++ b/solution.py
@@ -9,6 +9,7 @@
 
 DILATION = 4
 LAND = 64.0
+MESH = pl.DeviceIdType.MESH
 GELU_A = 0.7978845608028654
 GELU_B = 0.044715 * GELU_A
 
@@ -87,8 +88,90 @@
     )(polar_rows, polar_owner, field, land_mask)
 
 
-def own_kernel(left_ref, own_ref, right_ref, taps_ref, gain_ref, up_ref, down_ref, out_ref):
-    lat_rows, cols, channels = own_ref.shape
+def exchange_kernel(
+    near_first,
+    coded_ref,
+    send_ref,
+    taps_ref,
+    gain_ref,
+    up_ref,
+    down_ref,
+    out_ref,
+    mixed_ref,
+    left,
+    right,
+    pieces,
+    send_sem,
+    piece_sem,
+    halo_sem,
+):
+    lat_rows, cols, channels = coded_ref.shape
+    owners, slots = send_ref.shape[:2]
+    group = 8
+    groups = owners // group
+    band = lax.axis_index("lat")
+    me = lax.axis_index("lon")
+    mine, low = lax.div(me, group), lax.rem(me, group)
+    ahead, behind = lax.rem(me + 1, owners), lax.rem(me + owners - 1, owners)
+    shift = groups // 2 if near_first else 0
+
+    def span(tile, tiles):
+        return pl.ds(pl.multiple_of(tile * cols, cols), tiles * cols)
+
+    def piece_copy(position, other):
+        relative = lax.rem(position - shift + groups, groups)
+        target = lax.rem(mine - relative + groups, groups) * group + lax.rem(low + other, group)
+        return pltpu.make_async_remote_copy(
+            src_ref=send_ref.at[target],
+            dst_ref=pieces.at[:, span(position * group + low, 1)],
+            send_sem=send_sem.at[0],
+            recv_sem=piece_sem.at[position],
+            device_id=(band, target),
+            device_id_type=MESH,
+        )
+
+    def halo_copy(side, target, k):
+        return pltpu.make_async_remote_copy(
+            src_ref=coded_ref,
+            dst_ref=side,
+            send_sem=send_sem.at[1 + k],
+            recv_sem=halo_sem.at[k],
+            device_id=(band, target),
+            device_id_type=MESH,
+        )
+
+    barrier = pltpu.get_barrier_semaphore()
+
+    @pl.loop(1, owners)
+    def _(i):
+        pl.semaphore_signal(
+            barrier,
+            inc=1,
+            device_id=(band, lax.rem(me + i, owners)),
+            device_id_type=MESH,
+        )
+
+    own_position = shift if near_first else groups
+    pieces[:, span(own_position * group + low, 1)] = send_ref[me]
+    pl.semaphore_wait(barrier, owners - 1)
+
+    to_ahead = halo_copy(left, ahead, 0)
+    to_behind = halo_copy(right, behind, 1)
+    to_ahead.start()
+    to_behind.start()
+    middle = groups // 2
+    order = [middle]
+    for q in range(1, middle):
+        order += [middle - q, middle + q]
+    order += [groups]
+    for position in order:
+
+        @pl.loop(1 if position == own_position else 0, group)
+        def _(other, position=position):
+            piece_copy(position, other).start()
+
+    to_ahead.wait_recv()
+    to_behind.wait_recv()
     step = 8
 
     @pl.loop(0, lat_rows // step)
@@ -97,72 +180,112 @@
         tiles = jnp.concatenate(
             [
                 ref[rows].astype(jnp.float32).reshape(step, cols // 8, 8, channels)
-                for ref in (left_ref, own_ref, right_ref)
+                for ref in (left, coded_ref, right)
             ],
             axis=1,
         )
         mixed = mix(tiles, cols // 8, taps_ref, gain_ref[...], up_ref[...], down_ref[...])
         out_ref[rows] = mixed.reshape(step, cols, channels)
 
-
-def own(left, coded, right, taps, gain, up, down):
+    def arrived(position, tiles):
+        landed = pieces.at[:, span(position * group, tiles)]
+        pltpu.make_async_copy(landed, landed, piece_sem.at[position]).wait()
+
+    chunk = 4
+
+    def mix_chunk(tile):
+        keep = chunk * cols // 8
+        tiles = pieces[:, span(tile - 1, chunk + 2)].astype(jnp.float32)
+        tiles = tiles.reshape(slots, keep + 8, 8, channels)
+        mixed = mix(tiles, keep, taps_ref, gain_ref[...], up_ref[...], down_ref[...])
+        mixed_ref[:, span(tile, chunk)] = mixed.reshape(slots, chunk * cols, channels)
+
+    arrived(middle, group - 1 if own_position == middle else group)
+    mix_chunk(middle * group + 2)
+
+    @pl.loop(1, middle)
+    def _(q):
+        arrived(middle - q, group)
+        arrived(middle + q, group)
+
+        @pl.loop(0, 4)
+        def _(k):
+            side = lax.div(k, 2)
+            first = side * (middle * group + 6 + (q - 1) * group)
+            first += (1 - side) * (middle * group + 2 - q * group)
+            mix_chunk(first + lax.rem(k, 2) * chunk)
+
+    arrived(groups, group - 1 if own_position == groups else group)
+    ring = owners
+    pieces[:, span(group + ring, 3)] = pieces[:, span(group, 3)]
+
+    @pl.loop(0, 3)
+    def _(k):
+        mix_chunk(group + ring - 10 + k * chunk)
+
+    mixed_ref[:, span(ring + 10, 3)] = mixed_ref[:, span(10, 3)]
+
+    to_ahead.wait_send()
+    to_behind.wait_send()
+    sent = send_ref.at[pl.ds(0, owners - 1)]
+    pltpu.make_async_copy(sent, sent, send_sem.at[0]).wait()
+
+
+NEAR_FIRST = False
+
+
+def exchange(coded, outgoing, taps, gain, up, down):
+    owners, slots, cols, channels = outgoing.shape
     return pl.pallas_call(
-        own_kernel,
-        out_shape=jax.ShapeDtypeStruct(coded.shape, jnp.bfloat16),
-        in_specs=[vmem()] * 7,
-        out_specs=vmem(),
-    )(left, coded, right, taps, gain, up, down)
-
-
-def polar_kernel(raw_ref, taps_ref, gain_ref, up_ref, down_ref, line_ref, out_ref, padded, mixed):
-    tiles, slots, cols, channels = raw_ref.shape
-    length = tiles * cols
-    chunk = 256
+        functools.partial(exchange_kernel, NEAR_FIRST),
+        out_shape=(
+            jax.ShapeDtypeStruct(coded.shape, jnp.bfloat16),
+            jax.ShapeDtypeStruct((slots, (owners + 13) * cols, channels), jnp.bfloat16),
+        ),
+        in_specs=[vmem()] * 6,
+        out_specs=(vmem(), vmem()),
+        scratch_shapes=[
+            pltpu.VMEM(coded.shape, jnp.bfloat16),
+            pltpu.VMEM(coded.shape, jnp.bfloat16),
+            pltpu.VMEM((slots, (owners + 11) * cols, channels), jnp.bfloat16),
+            pltpu.SemaphoreType.DMA((3,)),
+            pltpu.SemaphoreType.DMA((9,)),
+            pltpu.SemaphoreType.DMA((2,)),
+        ],
+        compiler_params=pltpu.CompilerParams(collective_id=0, has_side_effects=True),
+    )(coded, outgoing, taps, gain, up, down)
+
+
+def filter_kernel(first_ref, mixed_ref, line_ref, out_ref):
+    slots, length, channels = out_ref.shape
+    cols = 32
     block = 128
     wide = block + 2 * cols
     band = pltpu.roll(jnp.broadcast_to(line_ref[...], (block, 256)), 0, 1, stride=1, stride_axis=0)
     band = band[:, :wide]
     high = band.astype(jnp.bfloat16)
     low = (band - high.astype(jnp.float32)).astype(jnp.bfloat16)
-    for s in range(slots):
-        padded[0:cols] = raw_ref[tiles - 1, s]
-        padded[cols + length : length + 2 * cols] = raw_ref[0, s]
-        padded[cols : cols + length] = raw_ref[:, s].reshape(length, channels)
-
-        @pl.loop(0, length // chunk)
-        def _(i):
-            at = pl.multiple_of(i * chunk, chunk)
-            tile = padded[pl.ds(at, chunk + 2 * cols)].astype(jnp.float32)
-            tile = tile.reshape(1, (chunk + 2 * cols) // 8, 8, channels)
-            mixed[pl.ds(cols + at, chunk)] = mix(
-                tile, chunk // 8, taps_ref, gain_ref[...], up_ref[...], down_ref[...]
-            )
-
-        mixed[0:cols] = mixed[length : length + cols]
-        mixed[cols + length : length + 2 * cols] = mixed[cols : 2 * cols]
-
-        @pl.loop(0, length // block)
-        def _(i):
-            at = pl.multiple_of(i * block, block)
-            window = mixed[pl.ds(at, wide)]
+    first = first_ref[0]
+
+    @pl.loop(0, length // block)
+    def _(i):
+        at = pl.multiple_of(lax.rem(first + i * block, length), block)
+        start = pl.multiple_of(11 * cols + i * block, cols)
+        for s in range(slots):
+            window = mixed_ref[s, pl.ds(start, wide)]
             total = jnp.dot(high, window, preferred_element_type=jnp.float32)
             total += jnp.dot(low, window, preferred_element_type=jnp.float32)
             out_ref[s, pl.ds(at, block)] = total.astype(jnp.bfloat16)
 
 
-def polar(raw, taps, gain, up, down, line):
-    tiles, slots, cols, channels = raw.shape
-    length = tiles * cols
+def polar_filter(first, mixed, line, length):
+    slots, _, channels = mixed.shape
     return pl.pallas_call(
-        polar_kernel,
+        filter_kernel,
         out_shape=jax.ShapeDtypeStruct((slots, length, channels), jnp.bfloat16),
-        in_specs=[vmem()] * 6,
+        in_specs=[smem(), vmem(), vmem()],
         out_specs=vmem(),
-        scratch_shapes=[
-            pltpu.VMEM((length + 2 * cols, channels), jnp.bfloat16),
-            pltpu.VMEM((length + 2 * cols, channels), jnp.bfloat16),
-        ],
-    )(raw, taps, gain, up, down, line)
+    )(first, mixed, line)
 
 
 def body(field, land_mask, taps, gain, up, down, polar_rows, polar_owner, polar_taps):
@@ -170,17 +293,15 @@
     slots = 2
     gain = gain[None, :]
     coded, outgoing = prepare(field, land_mask, polar_rows, polar_owner, owners, slots)
-    raw = lax.all_to_all(outgoing, "lon", split_axis=0, concat_axis=0, tiled=True)
-    ahead = [(i, (i + 1) % owners) for i in range(owners)]
-    back = [(i, (i - 1) % owners) for i in range(owners)]
-    left = lax.ppermute(coded, "lon", ahead)
-    right = lax.ppermute(coded, "lon", back)
-    mixed_field = own(left, coded, right, taps, gain, up, down)
+    mixed_field, mixed = exchange(coded, outgoing, taps, gain, up, down)
     cols = field.shape[1]
     half = polar_taps.shape[0] // 2
     line = jnp.zeros((1, 256), jnp.float32)
     line = lax.dynamic_update_slice(line, polar_taps[None, :], (0, cols - half))
-    polar_field = polar(raw, taps, gain, up, down, line)
+    length = owners * cols
+    place = lax.div(lax.axis_index("lon"), 8) * 8 + 12 + (owners // 2 if NEAR_FIRST else 0)
+    first = (lax.rem(place, owners) * cols)[None]
+    polar_field = polar_filter(first, mixed, line, length)
     return (mixed_field, polar_field)
 
 

time: 78.3 us -> 65.9 us (0.84)
  the two profiles are of different devices: /device:TPU:448 before, /device:TPU:15 now
where the time goes in v2:
time: 65.9 us; the launch traced here: 65.6 us
  Pallas kernels  62.1 us (94%)
  local copies, waits for them, and re-layouts  2.84 us (4%)
  between operations  0.68 us (1%)
    pallas_call x1, Pallas kernels, exchange(): pl.pallas_call(functools.partial(exchange_kernel, NEAR_FIRST), out_shape=...  52.8 us
    pallas_call x1, Pallas kernels, polar_filter(): pl.pallas_call(filter_kernel, out_shape=jax.ShapeDtypeStruct((slots, leng...  6.01 us
    pallas_call x1, Pallas kernels, prepare(): pl.pallas_call(prepare_kernel, out_shape=(jax.ShapeDtypeStruct(field.shap...  3.34 us
    unnamed x6, local copies, waits for them, and re-layouts  2.21 us

profile of v2, /device:TPU:15, one launch (start us, length us, event | category | flops | bytes accessed | tf_op | source)
XLA Modules:
  0.0 65.6 jit_solution(8234522342244248025)
XLA Ops:
  0.6 0.0 copy-start.1
  0.6 1.4 %copy.11.mask_ref = s32[64,32]{1,0:T(8,128)} copy(s32[64,32]{0,1:T(8,128)} %param.10) | data formatting | bytes 16384 | tf_op args[1]
  2.0 3.3 %shard_map.104 = (bf16[64,32,128]{2,1,0:T(8,128)(2,1)}, bf16[64,2,32,128]{3,2,1,0:T(8,128)(2,1)}) custom-call(s32[32]{0:T(128)} %rows_ref.1, s32[32]{0:T(128)} %owner_ref.1, bf16[64,32,128]{2,1,0:T(8,128)(2,1)} %field_ref.1, s32[64,32]{1,0:T(8,128)} %copy.11.mask_ref), custom_call_target="tpu_custom_call" | custom-call | tf_op jit(solution)/shard_map/pallas_call | solution.py:79
  5.4 52.8 %shard_map.105 = (bf16[64,32,128]{2,1,0:T(8,128)(2,1)}, bf16[2,2464,128]{2,1,0:T(8,128)(2,1)}) custom-call(bf16[64,32,128]{2,1,0:T(8,128)(2,1)} %get-tuple-element.6.coded_ref, bf16[64,2,32,128]{3,2,1,0:T(8,128)(2,1)} %get-tuple-element.7.send_ref, f32[15,128]{1,0:T(8,128)} %taps_ref.1, f32[1,128]{1,0:T(1,128)} %bitcast.4, bf16[128,512]{1,0:T(8,128)(2,1)} %up_ref.1, ...), custom_call_target="tpu_custom_call" | custom-call | tf_op jit(solution)/shard_map/pallas_call | solution.py:239
  58.2 0.0 copy-start
  58.2 0.0 copy-done.1
  58.2 0.6 dynamic_update_slice.3.line_ref
  58.8 6.0 %shard_map.106 = bf16[2,2048,128]{2,1,0:T(8,128)(2,1)} custom-call(s32[1]{0:T(128)} %bitcast.1.first_ref, bf16[2,2464,128]{2,1,0:T(8,128)(2,1)} %get-tuple-element.9.mixed_ref, f32[1,256]{1,0:T(1,128)} %dynamic_update_slice.3.line_ref), custom_call_target="tpu_custom_call" | custom-call | tf_op jit(solution)/shard_map/pallas_call | solution.py:283
  64.8 0.0 copy-done
  64.8 0.8 %copy.13 = bf16[64,32,128]{2,1,0:T(8,128)(2,1)} copy(bf16[64,32,128]{2,1,0:T(8,128)(2,1)S(1)} %copy-done) | data formatting | bytes 1048576
Async XLA Ops:
  0.6 57.5 %copy-start.1 = (f32[31]{0:T(128)S(1)}, f32[31]{0:T(128)}, u32[]{:S(2)}) copy-start(f32[31]{0:T(128)} %param.17) | copy-start | bytes 376
  58.2 6.7 %copy-start = (bf16[64,32,128]{2,1,0:T(8,128)(2,1)S(1)}, bf16[64,32,128]{2,1,0:T(8,128)(2,1)}, u32[]{:S(2)}) copy-start(bf16[64,32,128]{2,1,0:T(8,128)(2,1)} %get-tuple-element.12) | copy-start | bytes 1572868

commit v3 on v0

v3 whole, which is shorter than its diff:
```python
import jax
import jax.numpy as jnp
from jax import lax
from jax.experimental import pallas as pl
from jax.experimental.pallas import tpu as pltpu
from jax.sharding import PartitionSpec as P

MESH = pl.DeviceIdType.MESH
DILATION = 4
LAND = 64.0
GELU_A = 0.7978845608028654
GELU_B = 0.044715 * GELU_A
GROUP = 8
CHUNK = 4
SLOTS = 2


def mix(tiles, land, keep, taps, gain, half_up, down):
    rows, _, _, channels = tiles.shape
    turned = pltpu.roll(tiles.reshape(rows * (keep + 8), 8, channels), 4, 1).reshape(tiles.shape)
    first_half = lax.broadcasted_iota(jnp.int32, (rows, keep + 7, 8, channels), 2) < 4
    halves = jnp.where(first_half, turned[:, :-1], turned[:, 1:])
    zonal = None
    for k in range(taps.shape[0]):
        start = (k - 7) * DILATION + 32
        source = halves if start % 8 else tiles
        term = taps[k][None, None, None, :] * source[:, start // 8 : start // 8 + keep]
        zonal = term if zonal is None else zonal + term
    zonal = zonal.reshape(rows * keep * 8, channels)
    centred = zonal - jnp.mean(zonal, axis=-1, keepdims=True)
    variance = jnp.mean(centred * centred, axis=-1, keepdims=True)
    normed = (centred * lax.rsqrt(variance + 1e-06) * gain).astype(jnp.bfloat16)
    half = jnp.dot(normed, half_up, preferred_element_type=jnp.float32).astype(jnp.bfloat16)
    bend = half * (jnp.bfloat16(2 * GELU_A) + jnp.bfloat16(8 * GELU_B) * (half * half))
    hidden = half + half * jnp.tanh(bend)
    branch = jnp.dot(hidden, down, preferred_element_type=jnp.float32)
    mixed = tiles[:, 4 : 4 + keep].reshape(-1, channels) + branch
    return jnp.where(land.reshape(-1, channels), 0.0, mixed).astype(jnp.bfloat16)


def layer_kernel(
    table_ref,
    filter_ref,
    field_hbm,
    mask_hbm,
    taps_hbm,
    gain_hbm,
    up_hbm,
    down_hbm,
    out_hbm,
    polar_hbm,
    field,
    mask,
    taps,
    gain,
    up,
    down,
    coded,
    masked,
    left,
    right,
    outgoing,
    pieces,
    mixed,
    out,
    polar,
    load_sem,
    store_sem,
    send_sem,
    piece_sem,
    halo_sem,
):
    lat_rows, cols, channels = field.shape
    owners = outgoing.shape[0]
    groups = owners // GROUP
    middle = groups // 2
    band = lax.axis_index("lat")
    me = lax.axis_index("lon")
    mine, low = lax.div(me, GROUP), lax.rem(me, GROUP)
    ahead, behind = lax.rem(me + 1, owners), lax.rem(me + owners - 1, owners)

    loads = [
        pltpu.make_async_copy(source, target, load_sem.at[k])
        for k, (source, target) in enumerate(
            [
                (field_hbm, field),
                (mask_hbm, mask),
                (taps_hbm, taps),
                (gain_hbm, gain),
                (up_hbm, up),
                (down_hbm, down),
            ]
        )
    ]
    for load in loads:
        load.start()
    barrier = pltpu.get_barrier_semaphore()

    @pl.loop(1, owners)
    def _(i):
        pl.semaphore_signal(
            barrier,
            inc=1,
            device_id=(band, lax.rem(me + i, owners)),
            device_id_type=MESH,
        )

    def span(tile, tiles):
        return pl.ds(pl.multiple_of(tile * cols, cols), tiles * cols)

    def piece_copy(position, other):
        relative = lax.rem(position + middle, groups)
        target = lax.rem(mine - relative + groups, groups) * GROUP + lax.rem(low + other, GROUP)
        return pltpu.make_async_remote_copy(
            src_ref=outgoing.at[target],
            dst_ref=pieces.at[:, span(position * GROUP + low, 1)],
            send_sem=send_sem.at[0],
            recv_sem=piece_sem.at[position],
            device_id=(band, target),
            device_id_type=MESH,
        )

    def halo_copy(side, target, k):
        return pltpu.make_async_remote_copy(
            src_ref=masked,
            dst_ref=side,
            send_sem=send_sem.at[1 + k],
            recv_sem=halo_sem.at[k],
            device_id=(band, target),
            device_id_type=MESH,
        )

    loads[0].wait()
    loads[1].wait()
    for r in range(lat_rows):
        wet = jnp.broadcast_to(mask[:, r : r + 1], (cols, channels)) != 0
        values = field[r].astype(jnp.float32)
        coded[r] = jnp.where(wet, values, LAND).astype(jnp.bfloat16)
        masked[r] = jnp.where(wet, values, 0.0).astype(jnp.bfloat16)
    coded[lat_rows] = jnp.full((cols, channels), LAND, jnp.bfloat16)

    @pl.loop(0, owners // 4)
    def _(i):
        for j in range(4):
            for s in range(SLOTS):
                outgoing[i * 4 + j, s] = coded[table_ref[s * owners + i * 4 + j]]

    pieces[:, span(middle * GROUP + low, 1)] = outgoing[me]
    for load in loads[2:]:
        load.wait()
    half_up = (up[...].astype(jnp.float32) * 0.5).astype(jnp.bfloat16)
    up[...] = half_up

    pl.semaphore_wait(barrier, owners - 1)
    to_ahead = halo_copy(left, ahead, 0)
    to_behind = halo_copy(right, behind, 1)

    def send(position):
        @pl.loop(1 if position == middle else 0, GROUP)
        def _(other):
            piece_copy(position, other).start()

    send(middle)
    for q in range(1, middle):
        if q == middle - 1:
            to_ahead.start()
            to_behind.start()
        send(middle - q)
        send(middle + q)
    send(groups)

    def arrived(position, tiles):
        landed = pieces.at[:, span(position * GROUP, tiles)]
        pltpu.make_async_copy(landed, landed, piece_sem.at[position]).wait()

    def mix_chunk(tile):
        keep = CHUNK * cols // 8
        tiles = pieces[:, span(tile - 1, CHUNK + 2)].astype(jnp.float32)
        tiles = tiles.reshape(SLOTS, keep + 8, 8, channels)
        land = tiles == LAND
        tiles = jnp.where(land, 0.0, tiles)
        result = mix(tiles, land[:, 4 : 4 + keep], keep, taps, gain[...], up[...], down[...])
        mixed[:, span(tile, CHUNK)] = result.reshape(SLOTS, CHUNK * cols, channels)

    arrived(middle, GROUP - 1)
    mix_chunk(middle * GROUP + 2)
    step = 8
    store_own = pltpu.make_async_copy(out, out_hbm, store_sem.at[0])

    @pl.loop(1, middle)
    def _(q):
        @pl.when(q == middle - 1)
        def _():
            to_ahead.wait_recv()
            to_behind.wait_recv()

            @pl.loop(0, lat_rows // step)
            def _(i):
                rows = pl.ds(i * step, step)
                tiles = jnp.concatenate(
                    [
                        ref[rows].astype(jnp.float32).reshape(step, cols // 8, 8, channels)
                        for ref in (left, masked, right)
                    ],
                    axis=1,
                )
                keep = cols // 8
                land = coded[rows].astype(jnp.float32).reshape(step, keep, 8, channels) == LAND
                result = mix(tiles, land, keep, taps, gain[...], up[...], down[...])
                out[rows] = result.reshape(step, cols, channels)

            store_own.start()

        arrived(middle - q, GROUP)
        arrived(middle + q, GROUP)

        @pl.loop(0, 4)
        def _(k):
            side = lax.div(k, 2)
            first = side * (middle * GROUP + 6 + (q - 1) * GROUP)
            first += (1 - side) * (middle * GROUP + 2 - q * GROUP)
            mix_chunk(first + lax.rem(k, 2) * CHUNK)

    block = CHUNK * cols
    wide = block + 2 * cols
    lane = lax.broadcasted_iota(jnp.int32, (1, 256), 1)
    line = jnp.zeros((1, 256), jnp.float32)
    for k in range(filter_ref.shape[0]):
        line = jnp.where(lane == k + cols - filter_ref.shape[0] // 2, filter_ref[k], line)
    weights = pltpu.roll(jnp.broadcast_to(line, (block, 256)), 0, 1, stride=1, stride_axis=0)
    weights = weights[:, :wide]
    high = weights.astype(jnp.bfloat16)
    rest = (weights - high.astype(jnp.float32)).astype(jnp.bfloat16)
    place = mine * GROUP + middle * GROUP + 12

    def store_block(i):
        at = pl.multiple_of(lax.rem(place + i * CHUNK, owners) * cols, block)
        return pltpu.make_async_copy(
            polar.at[:, span(i * CHUNK, CHUNK)], polar_hbm.at[:, pl.ds(at, block)], store_sem.at[1]
        )

    def filter_blocks(begin, end):
        @pl.loop(begin, end)
        def _(i):
            window = mixed[:, span(11 + i * CHUNK, CHUNK + 2)]
            window = jnp.concatenate([window[s] for s in range(SLOTS)], axis=1)
            total = jnp.dot(high, window, preferred_element_type=jnp.float32)
            total += jnp.dot(rest, window, preferred_element_type=jnp.float32)
            total = total.astype(jnp.bfloat16)
            for s in range(SLOTS):
                polar[s, span(i * CHUNK, CHUNK)] = total[:, s * channels : (s + 1) * channels]
            store_block(i).start()

    blocks = owners // CHUNK
    filter_blocks(0, blocks - 4)
    arrived(groups, GROUP)
    pieces[:, span(GROUP + owners, 3)] = pieces[:, span(GROUP, 3)]

    @pl.loop(0, 3)
    def _(k):
        mix_chunk(GROUP + owners - 10 + k * CHUNK)

    mixed[:, span(owners + 10, 3)] = mixed[:, span(10, 3)]
    filter_blocks(blocks - 4, blocks)

    to_ahead.wait_send()
    to_behind.wait_send()
    sent = outgoing.at[pl.ds(0, owners - 1)]
    pltpu.make_async_copy(sent, sent, send_sem.at[0]).wait()
    store_own.wait()
    pltpu.make_async_copy(polar, polar_hbm, store_sem.at[1]).wait()


def layer(table, polar_taps, field, mask, taps, gain, up, down, owners):
    lat_rows, cols, channels = field.shape
    length = owners * cols
    smem = pl.BlockSpec(memory_space=pltpu.SMEM)
    anywhere = pl.BlockSpec(memory_space=pl.ANY)
    tile = pltpu.VMEM(field.shape, jnp.bfloat16)
    operands = (field, mask, taps, gain, up, down)
    return pl.pallas_call(
        layer_kernel,
        out_shape=(
            jax.ShapeDtypeStruct(field.shape, jnp.bfloat16),
            jax.ShapeDtypeStruct((SLOTS, length, channels), jnp.bfloat16),
        ),
        in_specs=[smem] * 2 + [anywhere] * 6,
        out_specs=(anywhere, anywhere),
        scratch_shapes=[pltpu.VMEM(x.shape, x.dtype) for x in operands]
        + [
            pltpu.VMEM((lat_rows + 1, cols, channels), jnp.bfloat16),
            tile,
            tile,
            tile,
            pltpu.VMEM((owners, SLOTS, cols, channels), jnp.bfloat16),
            pltpu.VMEM((SLOTS, length + 11 * cols, channels), jnp.bfloat16),
            pltpu.VMEM((SLOTS, length + 13 * cols, channels), jnp.bfloat16),
            tile,
            pltpu.VMEM((SLOTS, length, channels), jnp.bfloat16),
            pltpu.SemaphoreType.DMA((len(operands),)),
            pltpu.SemaphoreType.DMA((2,)),
            pltpu.SemaphoreType.DMA((3,)),
            pltpu.SemaphoreType.DMA((9,)),
            pltpu.SemaphoreType.DMA((2,)),
        ],
        compiler_params=pltpu.CompilerParams(collective_id=0, has_side_effects=True),
    )(table, polar_taps, *operands)


def row_table(polar_rows, polar_owner, owners, none):
    entries = jnp.arange(polar_rows.shape[0], dtype=jnp.int32)
    same = (polar_owner[:, None] == polar_owner[None, :]) & (entries[None, :] < entries[:, None])
    rank = jnp.sum(same.astype(jnp.int32), axis=1)
    place = rank * owners + polar_owner
    places = jnp.arange(SLOTS * owners, dtype=jnp.int32)
    hit = place[None, :] == places[:, None]
    return none + jnp.sum(jnp.where(hit, polar_rows[None, :] - none, 0), axis=1)


def body(field, land_mask, taps, gain, up, down, polar_rows, polar_owner, polar_taps):
    owners = lax.axis_size("lon")
    table = row_table(polar_rows, polar_owner, owners, field.shape[0])
    return layer(table, polar_taps, field, land_mask.T, taps, gain[None, :], up, down, owners)


def solution(mesh):
    in_specs = (P("lat", "lon", None), P("lat", "lon"), P(), P(), P(), P(), P("lat"), P("lat"), P())
    out_specs = (P("lat", "lon", None), P(("lat", "lon"), None, None))
    return jax.shard_map(body, mesh=mesh, in_specs=in_specs, out_specs=out_specs, check_vma=False)
```

time: 139 us -> 53.7 us (0.39)
  the two profiles are of different devices: /device:TPU:1 before, /device:TPU:24 now
where the time goes in v3:
time: 53.7 us; the launch traced here: 53.5 us
  Pallas kernels  48 us (89%)
  local copies, waits for them, and re-layouts  4.06 us (8%)
  other arithmetic  0.79 us (1%)
  between operations  0.66 us (1%)
    pallas_call x1, Pallas kernels, layer(): pl.pallas_call(layer_kernel, out_shape=(jax.ShapeDtypeStruct(field.shape,...  48 us
    unnamed x8, local copies, waits for them, and re-layouts  4.06 us

profile of v3, /device:TPU:24, one launch (start us, length us, event | category | flops | bytes accessed | tf_op | source)
XLA Modules:
  0.0 53.5 jit_solution(13478160273954775728)
XLA Ops:
  0.6 0.0 copy-start.1
  0.6 0.6 %copy-done.1 = s32[32]{0:T(128)S(1)} copy-done((s32[32]{0:T(128)S(1)}, s32[32]{0:T(128)}, u32[]{:S(2)}) %copy-start.1) | copy-done | bytes 152
  1.3 0.0 copy-start.2
  1.3 0.2 convert_reduce_fusion
  1.5 0.5 copy-done.2
  1.9 0.1 select_reduce_fusion
  2.0 0.5 broadcast_add_fusion.table_ref
  2.6 48.0 %shard_map.104 = (bf16[64,32,128]{2,1,0:T(8,128)(2,1)}, bf16[2,2048,128]{2,1,0:T(8,128)(2,1)}) custom-call(s32[128]{0:T(128)} %broadcast_add_fusion.table_ref, f32[31]{0:T(128)} %filter_ref.1, bf16[64,32,128]{2,1,0:T(8,128)(2,1)} %field_hbm.1, s32[32,64]{1,0:T(8,128)} %bitcast.2, f32[15,128]{1,0:T(8,128)} %taps_hbm.1, f32[1,128]{1,0:T(1,128)} %bitcast.3, ...), custom_call_target="tpu_custom_call" | custom-call | tf_op jit(solution)/shard_map/pallas_call | solution.py:281
  50.6 0.0 copy-start
  50.6 2.0 %copy.13 = bf16[64,32,128]{2,1,0:T(8,128)(2,1)} copy(bf16[64,32,128]{2,1,0:T(8,128)(2,1)} %get-tuple-element.6) | data formatting | bytes 1048576
  52.5 0.0 copy-done
  52.6 1.0 %copy.14 = bf16[2,2048,128]{2,1,0:T(8,128)(2,1)} copy(bf16[2,2048,128]{2,1,0:T(8,128)(2,1)S(1)} %copy-done) | data formatting | bytes 2097152
  (1 shorter events, 0.0 us)
Async XLA Ops:
  0.6 0.7 %copy-start.1 = (s32[32]{0:T(128)S(1)}, s32[32]{0:T(128)}, u32[]{:S(2)}) copy-start(s32[32]{0:T(128)} %param.16) | copy-start | bytes 388
  1.3 0.7 %copy-start.2 = (s32[32]{0:T(128)S(1)}, s32[32]{0:T(128)}, u32[]{:S(2)}) copy-start(s32[32]{0:T(128)} %param.15) | copy-start | bytes 388
  50.6 2.0 %copy-start = (bf16[2,2048,128]{2,1,0:T(8,128)(2,1)S(1)}, bf16[2,2048,128]{2,1,0:T(8,128)(2,1)}, u32[]{:S(2)}) copy-start(bf16[2,2048,128]{2,1,0:T(8,128)(2,1)} %get-tuple-element.7) | copy-start | bytes 3145732

commit v4 on v3

--- a/solution.py
+++ b/solution.py
@@ -30,31 +30,37 @@
     centred = zonal - jnp.mean(zonal, axis=-1, keepdims=True)
     variance = jnp.mean(centred * centred, axis=-1, keepdims=True)
     normed = (centred * lax.rsqrt(variance + 1e-06) * gain).astype(jnp.bfloat16)
-    half = jnp.dot(normed, half_up, preferred_element_type=jnp.float32).astype(jnp.bfloat16)
-    bend = half * (jnp.bfloat16(2 * GELU_A) + jnp.bfloat16(8 * GELU_B) * (half * half))
-    hidden = half + half * jnp.tanh(bend)
-    branch = jnp.dot(hidden, down, preferred_element_type=jnp.float32)
-    mixed = tiles[:, 4 : 4 + keep].reshape(-1, channels) + branch
+    half = jnp.dot(normed, half_up, preferred_element_type=jnp.float32)
+    bend = half * (2 * GELU_A + 8 * GELU_B * (half * half))
+    hidden = (half + half * jnp.tanh(bend)).astype(jnp.bfloat16)
+    branch = jnp.dot(hidden, down, preferred_element_type=jnp.float32).astype(jnp.bfloat16)
+    mixed = tiles[:, 4 : 4 + keep].reshape(-1, channels) + branch.astype(jnp.float32)
     return jnp.where(land.reshape(-1, channels), 0.0, mixed).astype(jnp.bfloat16)
 
 
 def layer_kernel(
-    table_ref,
-    filter_ref,
+    rows_hbm,
+    owner_hbm,
+    filter_hbm,
     field_hbm,
     mask_hbm,
     taps_hbm,
     gain_hbm,
     up_hbm,
     down_hbm,
-    out_hbm,
-    polar_hbm,
+    out_result,
+    polar_result,
+    listed,
+    owner,
+    filter_ref,
     field,
     mask,
     taps,
     gain,
     up,
     down,
+    table,
+    table_ref,
     coded,
     masked,
     left,
@@ -83,8 +89,11 @@
         pltpu.make_async_copy(source, target, load_sem.at[k])
         for k, (source, target) in enumerate(
             [
+                (rows_hbm, listed),
+                (owner_hbm, owner),
+                (mask_hbm, mask),
                 (field_hbm, field),
-                (mask_hbm, mask),
+                (filter_hbm, filter_ref),
                 (taps_hbm, taps),
                 (gain_hbm, gain),
                 (up_hbm, up),
@@ -92,18 +101,17 @@
             ]
         )
     ]
+    barrier = pltpu.get_barrier_semaphore()
+
+    @pl.loop(0, owners // 7)
+    def _(i):
+        for j in range(7):
+            other = lax.rem(me + owners // 2 + 1 + i * 7 + j, owners)
+            other = lax.rem(other + jnp.where(other == me, owners // 2, 0), owners)
+            pl.semaphore_signal(barrier, inc=1, device_id=(band, other), device_id_type=MESH)
+
     for load in loads:
         load.start()
-    barrier = pltpu.get_barrier_semaphore()
-
-    @pl.loop(1, owners)
-    def _(i):
-        pl.semaphore_signal(
-            barrier,
-            inc=1,
-            device_id=(band, lax.rem(me + i, owners)),
-            device_id_type=MESH,
-        )
 
     def span(tile, tiles):
         return pl.ds(pl.multiple_of(tile * cols, cols), tiles * cols)
@@ -132,6 +140,26 @@
 
     loads[0].wait()
     loads[1].wait()
+    entries = listed.shape[1]
+    shape = (entries, entries)
+    entry, earlier = (lax.broadcasted_iota(jnp.int32, shape, k) for k in range(2))
+    owners_along = jnp.broadcast_to(owner[...], shape).astype(jnp.float32)
+    rows_along = jnp.broadcast_to(listed[...], shape).astype(jnp.float32)
+
+    def total(keep, values):
+        return jnp.sum(jnp.where(keep, values, 0.0), axis=1, keepdims=True)
+
+    owner_of = total(entry == earlier, owners_along)
+    row_of = total(entry == earlier, rows_along).astype(jnp.int32)
+    rank = total((owners_along == owner_of) & (earlier < entry), jnp.ones(shape, jnp.float32))
+    place_of = (rank * owners + owner_of).astype(jnp.int32)
+    slot = lax.broadcasted_iota(jnp.int32, (entries, SLOTS * owners), 1)
+    fill = jnp.where(place_of == slot, row_of - lat_rows, 0)
+    table[...] = lat_rows + jnp.sum(fill, axis=0, keepdims=True)
+    to_scalars = pltpu.make_async_copy(table, table_ref, store_sem.at[0])
+    to_scalars.start()
+    loads[2].wait()
+    loads[3].wait()
     for r in range(lat_rows):
         wet = jnp.broadcast_to(mask[:, r : r + 1], (cols, channels)) != 0
         values = field[r].astype(jnp.float32)
@@ -139,14 +167,16 @@
         masked[r] = jnp.where(wet, values, 0.0).astype(jnp.bfloat16)
     coded[lat_rows] = jnp.full((cols, channels), LAND, jnp.bfloat16)
 
+    to_scalars.wait()
+
     @pl.loop(0, owners // 4)
     def _(i):
         for j in range(4):
             for s in range(SLOTS):
-                outgoing[i * 4 + j, s] = coded[table_ref[s * owners + i * 4 + j]]
+                outgoing[i * 4 + j, s] = coded[table_ref[0, s * owners + i * 4 + j]]
 
     pieces[:, span(middle * GROUP + low, 1)] = outgoing[me]
-    for load in loads[2:]:
+    for load in loads[4:]:
         load.wait()
     half_up = (up[...].astype(jnp.float32) * 0.5).astype(jnp.bfloat16)
     up[...] = half_up
@@ -173,19 +203,19 @@
         landed = pieces.at[:, span(position * GROUP, tiles)]
         pltpu.make_async_copy(landed, landed, piece_sem.at[position]).wait()
 
-    def mix_chunk(tile):
-        keep = CHUNK * cols // 8
-        tiles = pieces[:, span(tile - 1, CHUNK + 2)].astype(jnp.float32)
+    def mix_chunk(tile, tiles_wide):
+        keep = tiles_wide * cols // 8
+        tiles = pieces[:, span(tile - 1, tiles_wide + 2)].astype(jnp.float32)
         tiles = tiles.reshape(SLOTS, keep + 8, 8, channels)
         land = tiles == LAND
         tiles = jnp.where(land, 0.0, tiles)
         result = mix(tiles, land[:, 4 : 4 + keep], keep, taps, gain[...], up[...], down[...])
-        mixed[:, span(tile, CHUNK)] = result.reshape(SLOTS, CHUNK * cols, channels)
+        mixed[:, span(tile, tiles_wide)] = result.reshape(SLOTS, tiles_wide * cols, channels)
 
     arrived(middle, GROUP - 1)
-    mix_chunk(middle * GROUP + 2)
-    step = 8
-    store_own = pltpu.make_async_copy(out, out_hbm, store_sem.at[0])
+    mix_chunk(middle * GROUP + 2, 4)
+    step = 16
+    store_own = pltpu.make_async_copy(out, out_result, store_sem.at[0])
 
     @pl.loop(1, middle)
     def _(q):
@@ -214,19 +244,18 @@
         arrived(middle - q, GROUP)
         arrived(middle + q, GROUP)
 
-        @pl.loop(0, 4)
-        def _(k):
-            side = lax.div(k, 2)
+        @pl.loop(0, 2)
+        def _(side):
             first = side * (middle * GROUP + 6 + (q - 1) * GROUP)
             first += (1 - side) * (middle * GROUP + 2 - q * GROUP)
-            mix_chunk(first + lax.rem(k, 2) * CHUNK)
+            mix_chunk(first, GROUP)
 
     block = CHUNK * cols
     wide = block + 2 * cols
     lane = lax.broadcasted_iota(jnp.int32, (1, 256), 1)
     line = jnp.zeros((1, 256), jnp.float32)
-    for k in range(filter_ref.shape[0]):
-        line = jnp.where(lane == k + cols - filter_ref.shape[0] // 2, filter_ref[k], line)
+    for k in range(filter_ref.shape[1]):
+        line = jnp.where(lane == k + cols - filter_ref.shape[1] // 2, filter_ref[0, k], line)
     weights = pltpu.roll(jnp.broadcast_to(line, (block, 256)), 0, 1, stride=1, stride_axis=0)
     weights = weights[:, :wide]
     high = weights.astype(jnp.bfloat16)
@@ -236,7 +265,7 @@
     def store_block(i):
         at = pl.multiple_of(lax.rem(place + i * CHUNK, owners) * cols, block)
         return pltpu.make_async_copy(
-            polar.at[:, span(i * CHUNK, CHUNK)], polar_hbm.at[:, pl.ds(at, block)], store_sem.at[1]
+            polar.at[:, span(i * CHUNK, CHUNK)], polar_result.at[:, pl.ds(at, block)], store_sem.at[1]
         )
 
     def filter_blocks(begin, end):
@@ -256,9 +285,7 @@
     arrived(groups, GROUP)
     pieces[:, span(GROUP + owners, 3)] = pieces[:, span(GROUP, 3)]
 
-    @pl.loop(0, 3)
-    def _(k):
-        mix_chunk(GROUP + owners - 10 + k * CHUNK)
+    mix_chunk(GROUP + owners - 10, 12)
 
     mixed[:, span(owners + 10, 3)] = mixed[:, span(10, 3)]
     filter_blocks(blocks - 4, blocks)
@@ -268,26 +295,28 @@
     sent = outgoing.at[pl.ds(0, owners - 1)]
     pltpu.make_async_copy(sent, sent, send_sem.at[0]).wait()
     store_own.wait()
-    pltpu.make_async_copy(polar, polar_hbm, store_sem.at[1]).wait()
-
-
-def layer(table, polar_taps, field, mask, taps, gain, up, down, owners):
+    pltpu.make_async_copy(polar, polar_result, store_sem.at[1]).wait()
+
+
+def layer(polar_rows, polar_owner, polar_taps, field, mask, taps, gain, up, down, owners):
     lat_rows, cols, channels = field.shape
     length = owners * cols
-    smem = pl.BlockSpec(memory_space=pltpu.SMEM)
-    anywhere = pl.BlockSpec(memory_space=pl.ANY)
     tile = pltpu.VMEM(field.shape, jnp.bfloat16)
-    operands = (field, mask, taps, gain, up, down)
+    operands = (polar_rows, polar_owner, polar_taps, field, mask, taps, gain, up, down)
+    held = [pltpu.VMEM(x.shape, x.dtype) for x in operands]
+    held[2] = pltpu.SMEM(polar_taps.shape, polar_taps.dtype)
     return pl.pallas_call(
         layer_kernel,
         out_shape=(
             jax.ShapeDtypeStruct(field.shape, jnp.bfloat16),
             jax.ShapeDtypeStruct((SLOTS, length, channels), jnp.bfloat16),
         ),
-        in_specs=[smem] * 2 + [anywhere] * 6,
-        out_specs=(anywhere, anywhere),
-        scratch_shapes=[pltpu.VMEM(x.shape, x.dtype) for x in operands]
+        in_specs=[pl.BlockSpec(memory_space=pltpu.HBM)] * len(operands),
+        out_specs=(pl.BlockSpec(memory_space=pl.ANY),) * 2,
+        scratch_shapes=held
         + [
+            pltpu.VMEM((1, SLOTS * owners), jnp.int32),
+            pltpu.SMEM((1, SLOTS * owners), jnp.int32),
             pltpu.VMEM((lat_rows + 1, cols, channels), jnp.bfloat16),
             tile,
             tile,
@@ -303,24 +332,38 @@
             pltpu.SemaphoreType.DMA((9,)),
             pltpu.SemaphoreType.DMA((2,)),
         ],
-        compiler_params=pltpu.CompilerParams(collective_id=0, has_side_effects=True),
-    )(table, polar_taps, *operands)
-
-
-def row_table(polar_rows, polar_owner, owners, none):
-    entries = jnp.arange(polar_rows.shape[0], dtype=jnp.int32)
-    same = (polar_owner[:, None] == polar_owner[None, :]) & (entries[None, :] < entries[:, None])
-    rank = jnp.sum(same.astype(jnp.int32), axis=1)
-    place = rank * owners + polar_owner
-    places = jnp.arange(SLOTS * owners, dtype=jnp.int32)
-    hit = place[None, :] == places[:, None]
-    return none + jnp.sum(jnp.where(hit, polar_rows[None, :] - none, 0), axis=1)
+        compiler_params=pltpu.CompilerParams(
+            collective_id=0, has_side_effects=True, vmem_limit_bytes=32 << 20
+        ),
+    )(*(pltpu.with_memory_space_constraint(x, pltpu.HBM) for x in operands))
+
+
+def write_kernel(field_ref, polar_ref, field_out, polar_out, sem):
+    copies = [
+        pltpu.make_async_copy(polar_ref, polar_out, sem.at[0]),
+        pltpu.make_async_copy(field_ref, field_out, sem.at[1]),
+    ]
+    for copy in copies:
+        copy.start()
+    for copy in copies:
+        copy.wait()
+
+
+def write(mixed_field, polar_field):
+    return pl.pallas_call(
+        write_kernel,
+        out_shape=tuple(jax.ShapeDtypeStruct(x.shape, x.dtype) for x in (mixed_field, polar_field)),
+        in_specs=[pl.BlockSpec(memory_space=pl.ANY)] * 2,
+        out_specs=(pl.BlockSpec(memory_space=pltpu.HBM),) * 2,
+        scratch_shapes=[pltpu.SemaphoreType.DMA((2,))],
+        compiler_params=pltpu.CompilerParams(vmem_limit_bytes=1 << 20),
+    )(mixed_field, polar_field)
 
 
 def body(field, land_mask, taps, gain, up, down, polar_rows, polar_owner, polar_taps):
     owners = lax.axis_size("lon")
-    table = row_table(polar_rows, polar_owner, owners, field.shape[0])
-    return layer(table, polar_taps, field, land_mask.T, taps, gain[None, :], up, down, owners)
+    lists = (polar_rows[None, :], polar_owner[None, :], polar_taps[None, :])
+    return write(*layer(*lists, field, land_mask.T, taps, gain[None, :], up, down, owners))
 
 
 def solution(mesh):

time: 53.7 us -> 48.4 us (0.901)
  the two profiles are of different devices: /device:TPU:24 before, /device:TPU:383 now
where the time goes in v4:
time: 48.4 us; the launch traced here: 48.3 us
  Pallas kernels  47.6 us (98%)
  between operations  0.64 us (1%)
    pallas_call x1, Pallas kernels, layer(): pl.pallas_call(layer_kernel, out_shape=(jax.ShapeDtypeStruct(field.shape,...  46.5 us
    pallas_call x1, Pallas kernels, write(): pl.pallas_call(write_kernel, out_shape=tuple((jax.ShapeDtypeStruct(x.shap...  1.16 us

profile of v4, /device:TPU:383, one launch (start us, length us, event | category | flops | bytes accessed | tf_op | source)
XLA Modules:
  0.0 48.3 jit_solution(4365062141499374836)
XLA Ops:
  0.6 46.5 %shard_map.104 = (bf16[64,32,128]{2,1,0:T(8,128)(2,1)S(1)}, bf16[2,2048,128]{2,1,0:T(8,128)(2,1)S(1)}) custom-call(s32[1,32]{1,0:T(1,128)} %bitcast.6, s32[1,32]{1,0:T(1,128)} %bitcast.7, f32[1,31]{1,0:T(1,128)} %bitcast.8, bf16[64,32,128]{2,1,0:T(8,128)(2,1)} %field_hbm.1, s32[32,64]{1,0:T(8,128)} %bitcast.5, f32[15,128]{1,0:T(8,128)} %taps_hbm.1, ...), custom_call_target="tpu_custom_call" | custom-call | tf_op jit(solution)/shard_map/pallas_call | solution.py:308
  47.1 1.2 %shard_map.105 = (bf16[64,32,128]{2,1,0:T(8,128)(2,1)}, bf16[2,2048,128]{2,1,0:T(8,128)(2,1)}) custom-call(bf16[64,32,128]{2,1,0:T(8,128)(2,1)S(1)} %get-tuple-element.4.field_ref, bf16[2,2048,128]{2,1,0:T(8,128)(2,1)S(1)} %get-tuple-element.5.polar_ref), custom_call_target="tpu_custom_call" | custom-call | tf_op jit(solution)/shard_map/pallas_call | solution.py:353

commit v5 on v4

--- a/solution.py
+++ b/solution.py
@@ -65,6 +65,7 @@
     masked,
     left,
     right,
+    passing,
     outgoing,
     pieces,
     mixed,
@@ -190,11 +191,71 @@
         def _(other):
             piece_copy(position, other).start()
 
+    parts = GROUP // 2
+    quarter = lat_rows // parts
+    column = lax.div(low, 2)
+
+    def rows_of(k):
+        return pl.ds(k * quarter, quarter)
+
+    def quarter_copy(k, side, step, k_side):
+        over = lax.rem(mine + step, groups) * GROUP
+        direct = k == (parts - 1 if k_side == 0 else 0)
+        target = over + (GROUP - 1 if k_side else 0) if direct else mine * GROUP + 2 * k + 1 - k_side
+        return pltpu.make_async_remote_copy(
+            src_ref=masked.at[rows_of(k)],
+            dst_ref=side.at[rows_of(k)] if direct else passing,
+            send_sem=send_sem.at[1 + k_side],
+            recv_sem=halo_sem.at[k_side] if direct else halo_sem.at[2],
+            device_id=(band, target),
+            device_id_type=MESH,
+        )
+
+    def hand_on(side, k_side):
+        return pltpu.make_async_remote_copy(
+            src_ref=passing,
+            dst_ref=side.at[rows_of(column)],
+            send_sem=send_sem.at[3],
+            recv_sem=halo_sem.at[k_side],
+            device_id=(
+                band,
+                lax.rem(mine + (groups - 1 if k_side else 1), groups) * GROUP
+                + (GROUP - 1 if k_side else 0),
+            ),
+            device_id_type=MESH,
+        )
+
+    first, final = low == 0, low == GROUP - 1
+    inner, outer = low != 0, low != GROUP - 1
+    odd = lax.rem(low, 2) == 1
+    hands_left = odd & (low < GROUP - 1)
+    hands_right = (lax.rem(low, 2) == 0) & (low > 0)
+    pass_left, pass_right = hand_on(left, 0), hand_on(right, 1)
+
+    @pl.when(final)
+    def _():
+        for k in range(parts):
+            quarter_copy(k, left, 1, 0).start()
+
+    @pl.when(first)
+    def _():
+        for k in range(parts):
+            quarter_copy(k, right, groups - 1, 1).start()
+
     send(middle)
-    for q in range(1, middle):
-        if q == middle - 1:
-            to_ahead.start()
-            to_behind.start()
+    for q in (1, 2):
+        send(middle - q)
+        send(middle + q)
+
+    @pl.when(hands_left | hands_right)
+    def _():
+        pltpu.make_async_copy(passing, passing, halo_sem.at[2]).wait()
+
+    pl.when(hands_left)(pass_left.start)
+    pl.when(hands_right)(pass_right.start)
+    pl.when(outer)(to_ahead.start)
+    pl.when(inner)(to_behind.start)
+    for q in range(3, middle):
         send(middle - q)
         send(middle + q)
     send(groups)
@@ -203,17 +264,17 @@
         landed = pieces.at[:, span(position * GROUP, tiles)]
         pltpu.make_async_copy(landed, landed, piece_sem.at[position]).wait()
 
-    def mix_chunk(tile, tiles_wide):
+    def mix_chunk(tile, tiles_wide, at=pl.ds(0, SLOTS)):
         keep = tiles_wide * cols // 8
-        tiles = pieces[:, span(tile - 1, tiles_wide + 2)].astype(jnp.float32)
-        tiles = tiles.reshape(SLOTS, keep + 8, 8, channels)
+        tiles = pieces[at, span(tile - 1, tiles_wide + 2)].astype(jnp.float32)
+        tiles = tiles.reshape(at.size, keep + 8, 8, channels)
         land = tiles == LAND
         tiles = jnp.where(land, 0.0, tiles)
         result = mix(tiles, land[:, 4 : 4 + keep], keep, taps, gain[...], up[...], down[...])
-        mixed[:, span(tile, tiles_wide)] = result.reshape(SLOTS, tiles_wide * cols, channels)
+        mixed[at, span(tile, tiles_wide)] = result.reshape(at.size, tiles_wide * cols, channels)
 
     arrived(middle, GROUP - 1)
-    mix_chunk(middle * GROUP + 2, 4)
+    mix_chunk(middle * GROUP + 1, GROUP - 2)
     step = 16
     store_own = pltpu.make_async_copy(out, out_result, store_sem.at[0])
 
@@ -246,8 +307,8 @@
 
         @pl.loop(0, 2)
         def _(side):
-            first = side * (middle * GROUP + 6 + (q - 1) * GROUP)
-            first += (1 - side) * (middle * GROUP + 2 - q * GROUP)
+            first = side * (middle * GROUP + 7 + (q - 1) * GROUP)
+            first += (1 - side) * (middle * GROUP + 1 - q * GROUP)
             mix_chunk(first, GROUP)
 
     block = CHUNK * cols
@@ -262,36 +323,49 @@
     rest = (weights - high.astype(jnp.float32)).astype(jnp.bfloat16)
     place = mine * GROUP + middle * GROUP + 12
 
-    def store_block(i):
-        at = pl.multiple_of(lax.rem(place + i * CHUNK, owners) * cols, block)
+    def store_block(i, at):
+        there = pl.multiple_of(lax.rem(place + i * CHUNK, owners) * cols, block)
         return pltpu.make_async_copy(
-            polar.at[:, span(i * CHUNK, CHUNK)], polar_result.at[:, pl.ds(at, block)], store_sem.at[1]
-        )
-
-    def filter_blocks(begin, end):
-        @pl.loop(begin, end)
-        def _(i):
-            window = mixed[:, span(11 + i * CHUNK, CHUNK + 2)]
-            window = jnp.concatenate([window[s] for s in range(SLOTS)], axis=1)
-            total = jnp.dot(high, window, preferred_element_type=jnp.float32)
-            total += jnp.dot(rest, window, preferred_element_type=jnp.float32)
-            total = total.astype(jnp.bfloat16)
-            for s in range(SLOTS):
-                polar[s, span(i * CHUNK, CHUNK)] = total[:, s * channels : (s + 1) * channels]
-            store_block(i).start()
+            polar.at[at, span(i * CHUNK, CHUNK)],
+            polar_result.at[at, pl.ds(there, block)],
+            store_sem.at[1],
+        )
+
+    def filtered(window):
+        total = jnp.dot(high, window, preferred_element_type=jnp.float32)
+        total += jnp.dot(rest, window, preferred_element_type=jnp.float32)
+        return total.astype(jnp.bfloat16)
 
     blocks = owners // CHUNK
-    filter_blocks(0, blocks - 4)
+    both = pl.ds(0, SLOTS)
+    pieces[:, span(GROUP + owners, 2)] = pieces[:, span(GROUP, 2)]
+    mixed[:, span(owners + 9, 4)] = mixed[:, span(9, 4)]
+
+    @pl.loop(0, blocks - 4)
+    def _(i):
+        window = mixed[:, span(11 + i * CHUNK, CHUNK + 2)]
+        result = filtered(jnp.concatenate([window[s] for s in range(SLOTS)], axis=1))
+        for s in range(SLOTS):
+            polar[s, span(i * CHUNK, CHUNK)] = result[:, s * channels : (s + 1) * channels]
+        store_block(i, both).start()
+
     arrived(groups, GROUP)
-    pieces[:, span(GROUP + owners, 3)] = pieces[:, span(GROUP, 3)]
-
-    mix_chunk(GROUP + owners - 10, 12)
-
-    mixed[:, span(owners + 10, 3)] = mixed[:, span(10, 3)]
-    filter_blocks(blocks - 4, blocks)
+    mix_chunk(owners - 1, GROUP + 2)
+    late = range(blocks - 4, blocks)
+    windows = [mixed[:, span(11 + i * CHUNK, CHUNK + 2)] for i in late]
+    windows = [window[s] for window in windows for s in range(SLOTS)]
+    result = filtered(jnp.concatenate(windows, axis=1))
+    for k, i in enumerate(late):
+        for s in range(SLOTS):
+            at = (k * SLOTS + s) * channels
+            polar[s, span(i * CHUNK, CHUNK)] = result[:, at : at + channels]
+    for i in late:
+        store_block(i, both).start()
 
     to_ahead.wait_send()
     to_behind.wait_send()
+    pl.when(hands_left)(pass_left.wait_send)
+    pl.when(hands_right)(pass_right.wait_send)
     sent = outgoing.at[pl.ds(0, owners - 1)]
     pltpu.make_async_copy(sent, sent, send_sem.at[0]).wait()
     store_own.wait()
@@ -321,6 +395,7 @@
             tile,
             tile,
             tile,
+            pltpu.VMEM((lat_rows // (GROUP // 2), cols, channels), jnp.bfloat16),
             pltpu.VMEM((owners, SLOTS, cols, channels), jnp.bfloat16),
             pltpu.VMEM((SLOTS, length + 11 * cols, channels), jnp.bfloat16),
             pltpu.VMEM((SLOTS, length + 13 * cols, channels), jnp.bfloat16),
@@ -328,9 +403,9 @@
             pltpu.VMEM((SLOTS, length, channels), jnp.bfloat16),
             pltpu.SemaphoreType.DMA((len(operands),)),
             pltpu.SemaphoreType.DMA((2,)),
+            pltpu.SemaphoreType.DMA((4,)),
+            pltpu.SemaphoreType.DMA((9,)),
             pltpu.SemaphoreType.DMA((3,)),
-            pltpu.SemaphoreType.DMA((9,)),
-            pltpu.SemaphoreType.DMA((2,)),
         ],
         compiler_params=pltpu.CompilerParams(
             collective_id=0, has_side_effects=True, vmem_limit_bytes=32 << 20
@@ -339,10 +414,17 @@
 
 
 def write_kernel(field_ref, polar_ref, field_out, polar_out, sem):
-    copies = [
-        pltpu.make_async_copy(polar_ref, polar_out, sem.at[0]),
-        pltpu.make_async_copy(field_ref, field_out, sem.at[1]),
-    ]
+    parts = sem.shape[0] // 3
+    wide, high = polar_ref.shape[1] // (2 * parts), field_ref.shape[0] // parts
+    copies = []
+    for k in range(2 * parts):
+        at = pl.ds(k * wide, wide)
+        copies.append(pltpu.make_async_copy(polar_ref.at[:, at], polar_out.at[:, at], sem.at[k]))
+    for k in range(parts):
+        at = pl.ds(k * high, high)
+        copies.append(
+            pltpu.make_async_copy(field_ref.at[at], field_out.at[at], sem.at[2 * parts + k])
+        )
     for copy in copies:
         copy.start()
     for copy in copies:
@@ -355,7 +437,7 @@
         out_shape=tuple(jax.ShapeDtypeStruct(x.shape, x.dtype) for x in (mixed_field, polar_field)),
         in_specs=[pl.BlockSpec(memory_space=pl.ANY)] * 2,
         out_specs=(pl.BlockSpec(memory_space=pltpu.HBM),) * 2,
-        scratch_shapes=[pltpu.SemaphoreType.DMA((2,))],
+        scratch_shapes=[pltpu.SemaphoreType.DMA((6,))],
         compiler_params=pltpu.CompilerParams(vmem_limit_bytes=1 << 20),
     )(mixed_field, polar_field)
 

time: 48.4 us -> 45.3 us (0.936)
  the two profiles are of different devices: /device:TPU:383 before, /device:TPU:1 now
where the time goes in v5:
time: 45.3 us; the launch traced here: 44.5 us
  Pallas kernels  43.9 us (97%)
  between operations  0.64 us (1%)
    pallas_call x1, Pallas kernels, layer(): pl.pallas_call(layer_kernel, out_shape=(jax.ShapeDtypeStruct(field.shape,...  42.7 us
    pallas_call x1, Pallas kernels, write(): pl.pallas_call(write_kernel, out_shape=tuple((jax.ShapeDtypeStruct(x.shap...  1.19 us

profile of v5, /device:TPU:1, one launch (start us, length us, event | category | flops | bytes accessed | tf_op | source)
XLA Modules:
  0.0 44.5 jit_solution(7403510282706963043)
XLA Ops:
  0.6 42.7 %shard_map.104 = (bf16[64,32,128]{2,1,0:T(8,128)(2,1)S(1)}, bf16[2,2048,128]{2,1,0:T(8,128)(2,1)S(1)}) custom-call(s32[1,32]{1,0:T(1,128)} %bitcast.6, s32[1,32]{1,0:T(1,128)} %bitcast.7, f32[1,31]{1,0:T(1,128)} %bitcast.8, bf16[64,32,128]{2,1,0:T(8,128)(2,1)} %field_hbm.1, s32[32,64]{1,0:T(8,128)} %bitcast.5, f32[15,128]{1,0:T(8,128)} %taps_hbm.1, ...), custom_call_target="tpu_custom_call" | custom-call | tf_op jit(solution)/shard_map/pallas_call | solution.py:382
  43.4 1.2 %shard_map.105 = (bf16[64,32,128]{2,1,0:T(8,128)(2,1)}, bf16[2,2048,128]{2,1,0:T(8,128)(2,1)}) custom-call(bf16[64,32,128]{2,1,0:T(8,128)(2,1)S(1)} %get-tuple-element.4.field_ref, bf16[2,2048,128]{2,1,0:T(8,128)(2,1)S(1)} %get-tuple-element.5.polar_ref), custom_call_target="tpu_custom_call" | custom-call | tf_op jit(solution)/shard_map/pallas_call | solution.py:435

commit v6 on v5

--- a/solution.py
+++ b/solution.py
@@ -69,8 +69,6 @@
     outgoing,
     pieces,
     mixed,
-    out,
-    polar,
     load_sem,
     store_sem,
     send_sem,
@@ -276,7 +274,6 @@
     arrived(middle, GROUP - 1)
     mix_chunk(middle * GROUP + 1, GROUP - 2)
     step = 16
-    store_own = pltpu.make_async_copy(out, out_result, store_sem.at[0])
 
     @pl.loop(1, middle)
     def _(q):
@@ -298,9 +295,7 @@
                 keep = cols // 8
                 land = coded[rows].astype(jnp.float32).reshape(step, keep, 8, channels) == LAND
                 result = mix(tiles, land, keep, taps, gain[...], up[...], down[...])
-                out[rows] = result.reshape(step, cols, channels)
-
-            store_own.start()
+                out_result[rows] = result.reshape(step, cols, channels)
 
         arrived(middle - q, GROUP)
         arrived(middle + q, GROUP)
@@ -323,13 +318,8 @@
     rest = (weights - high.astype(jnp.float32)).astype(jnp.bfloat16)
     place = mine * GROUP + middle * GROUP + 12
 
-    def store_block(i, at):
-        there = pl.multiple_of(lax.rem(place + i * CHUNK, owners) * cols, block)
-        return pltpu.make_async_copy(
-            polar.at[at, span(i * CHUNK, CHUNK)],
-            polar_result.at[at, pl.ds(there, block)],
-            store_sem.at[1],
-        )
+    def block_at(i):
+        return pl.ds(pl.multiple_of(lax.rem(place + i * CHUNK, owners) * cols, block), block)
 
     def filtered(window):
         total = jnp.dot(high, window, preferred_element_type=jnp.float32)
@@ -337,7 +327,6 @@
         return total.astype(jnp.bfloat16)
 
     blocks = owners // CHUNK
-    both = pl.ds(0, SLOTS)
     pieces[:, span(GROUP + owners, 2)] = pieces[:, span(GROUP, 2)]
     mixed[:, span(owners + 9, 4)] = mixed[:, span(9, 4)]
 
@@ -346,8 +335,7 @@
         window = mixed[:, span(11 + i * CHUNK, CHUNK + 2)]
         result = filtered(jnp.concatenate([window[s] for s in range(SLOTS)], axis=1))
         for s in range(SLOTS):
-            polar[s, span(i * CHUNK, CHUNK)] = result[:, s * channels : (s + 1) * channels]
-        store_block(i, both).start()
+            polar_result[s, block_at(i)] = result[:, s * channels : (s + 1) * channels]
 
     arrived(groups, GROUP)
     mix_chunk(owners - 1, GROUP + 2)
@@ -358,9 +346,7 @@
     for k, i in enumerate(late):
         for s in range(SLOTS):
             at = (k * SLOTS + s) * channels
-            polar[s, span(i * CHUNK, CHUNK)] = result[:, at : at + channels]
-    for i in late:
-        store_block(i, both).start()
+            polar_result[s, block_at(i)] = result[:, at : at + channels]
 
     to_ahead.wait_send()
     to_behind.wait_send()
@@ -368,8 +354,6 @@
     pl.when(hands_right)(pass_right.wait_send)
     sent = outgoing.at[pl.ds(0, owners - 1)]
     pltpu.make_async_copy(sent, sent, send_sem.at[0]).wait()
-    store_own.wait()
-    pltpu.make_async_copy(polar, polar_result, store_sem.at[1]).wait()
 
 
 def layer(polar_rows, polar_owner, polar_taps, field, mask, taps, gain, up, down, owners):
@@ -386,7 +370,7 @@
             jax.ShapeDtypeStruct((SLOTS, length, channels), jnp.bfloat16),
         ),
         in_specs=[pl.BlockSpec(memory_space=pltpu.HBM)] * len(operands),
-        out_specs=(pl.BlockSpec(memory_space=pl.ANY),) * 2,
+        out_specs=(pl.BlockSpec(memory_space=pltpu.VMEM),) * 2,
         scratch_shapes=held
         + [
             pltpu.VMEM((1, SLOTS * owners), jnp.int32),
@@ -399,10 +383,8 @@
             pltpu.VMEM((owners, SLOTS, cols, channels), jnp.bfloat16),
             pltpu.VMEM((SLOTS, length + 11 * cols, channels), jnp.bfloat16),
             pltpu.VMEM((SLOTS, length + 13 * cols, channels), jnp.bfloat16),
-            tile,
-            pltpu.VMEM((SLOTS, length, channels), jnp.bfloat16),
             pltpu.SemaphoreType.DMA((len(operands),)),
-            pltpu.SemaphoreType.DMA((2,)),
+            pltpu.SemaphoreType.DMA((1,)),
             pltpu.SemaphoreType.DMA((4,)),
             pltpu.SemaphoreType.DMA((9,)),
             pltpu.SemaphoreType.DMA((3,)),

time: 45.3 us -> 44.6 us (0.985)
  Pallas kernels: 43.9 us -> 43.1 us
    pallas_call x1, Pallas kernels: 42.7 us -> 42 us  [layer(): pl.pallas_call(layer_kernel, out_shape=(jax.ShapeDtypeStruct(field.shape,...]
where the time goes in v6:
time: 44.6 us; the launch traced here: 43.8 us
  Pallas kernels  43.1 us (97%)
  between operations  0.64 us (1%)
    pallas_call x1, Pallas kernels, layer(): pl.pallas_call(layer_kernel, out_shape=(jax.ShapeDtypeStruct(field.shape,...  42 us
    pallas_call x1, Pallas kernels, write(): pl.pallas_call(write_kernel, out_shape=tuple((jax.ShapeDtypeStruct(x.shap...  1.19 us

profile of v6, /device:TPU:1, one launch (start us, length us, event | category | flops | bytes accessed | tf_op | source)
XLA Modules:
  0.0 43.8 jit_solution(14553696796583956028)
XLA Ops:
  0.6 42.0 %shard_map.104 = (bf16[64,32,128]{2,1,0:T(8,128)(2,1)S(1)}, bf16[2,2048,128]{2,1,0:T(8,128)(2,1)S(1)}) custom-call(s32[1,32]{1,0:T(1,128)} %bitcast.6, s32[1,32]{1,0:T(1,128)} %bitcast.7, f32[1,31]{1,0:T(1,128)} %bitcast.8, bf16[64,32,128]{2,1,0:T(8,128)(2,1)} %field_hbm.1, s32[32,64]{1,0:T(8,128)} %bitcast.5, f32[15,128]{1,0:T(8,128)} %taps_hbm.1, ...), custom_call_target="tpu_custom_call" | custom-call | tf_op jit(solution)/shard_map/pallas_call | solution.py:366
  42.6 1.2 %shard_map.105 = (bf16[64,32,128]{2,1,0:T(8,128)(2,1)}, bf16[2,2048,128]{2,1,0:T(8,128)(2,1)}) custom-call(bf16[64,32,128]{2,1,0:T(8,128)(2,1)S(1)} %get-tuple-element.4.field_ref, bf16[2,2048,128]{2,1,0:T(8,128)(2,1)S(1)} %get-tuple-element.5.polar_ref), custom_call_target="tpu_custom_call" | custom-call | tf_op jit(solution)/shard_map/pallas_call | solution.py:417

commit v7 on v6

--- a/solution.py
+++ b/solution.py
@@ -174,12 +174,6 @@
             for s in range(SLOTS):
                 outgoing[i * 4 + j, s] = coded[table_ref[0, s * owners + i * 4 + j]]
 
-    pieces[:, span(middle * GROUP + low, 1)] = outgoing[me]
-    for load in loads[4:]:
-        load.wait()
-    half_up = (up[...].astype(jnp.float32) * 0.5).astype(jnp.bfloat16)
-    up[...] = half_up
-
     pl.semaphore_wait(barrier, owners - 1)
     to_ahead = halo_copy(left, ahead, 0)
     to_behind = halo_copy(right, behind, 1)
@@ -257,6 +251,11 @@
         send(middle - q)
         send(middle + q)
     send(groups)
+    pieces[:, span(middle * GROUP + low, 1)] = outgoing[me]
+    for load in loads[4:]:
+        load.wait()
+    half_up = (up[...].astype(jnp.float32) * 0.5).astype(jnp.bfloat16)
+    up[...] = half_up
 
     def arrived(position, tiles):
         landed = pieces.at[:, span(position * GROUP, tiles)]
@@ -270,6 +269,32 @@
         tiles = jnp.where(land, 0.0, tiles)
         result = mix(tiles, land[:, 4 : 4 + keep], keep, taps, gain[...], up[...], down[...])
         mixed[at, span(tile, tiles_wide)] = result.reshape(at.size, tiles_wide * cols, channels)
+
+    block = CHUNK * cols
+    wide = block + 2 * cols
+    lane = lax.broadcasted_iota(jnp.int32, (1, 256), 1)
+    line = jnp.zeros((1, 256), jnp.float32)
+    for k in range(filter_ref.shape[1]):
+        line = jnp.where(lane == k + cols - filter_ref.shape[1] // 2, filter_ref[0, k], line)
+    weights = pltpu.roll(jnp.broadcast_to(line, (block, 256)), 0, 1, stride=1, stride_axis=0)
+    weights = weights[:, :wide]
+    high = weights.astype(jnp.bfloat16)
+    rest = (weights - high.astype(jnp.float32)).astype(jnp.bfloat16)
+    place = mine * GROUP + middle * GROUP + 12
+
+    def block_at(i):
+        return pl.ds(pl.multiple_of(lax.rem(place + i * CHUNK, owners) * cols, block), block)
+
+    def filtered(window):
+        total = jnp.dot(high, window, preferred_element_type=jnp.float32)
+        total += jnp.dot(rest, window, preferred_element_type=jnp.float32)
+        return total.astype(jnp.bfloat16)
+
+    def filter_block(i):
+        window = mixed[:, span(11 + i * CHUNK, CHUNK + 2)]
+        result = filtered(jnp.concatenate([window[s] for s in range(SLOTS)], axis=1))
+        for s in range(SLOTS):
+            polar_result[s, block_at(i)] = result[:, s * channels : (s + 1) * channels]
 
     arrived(middle, GROUP - 1)
     mix_chunk(middle * GROUP + 1, GROUP - 2)
@@ -297,6 +322,8 @@
                 result = mix(tiles, land, keep, taps, gain[...], up[...], down[...])
                 out_result[rows] = result.reshape(step, cols, channels)
 
+            pl.loop(2, 10)(filter_block)
+
         arrived(middle - q, GROUP)
         arrived(middle + q, GROUP)
 
@@ -306,36 +333,13 @@
             first += (1 - side) * (middle * GROUP + 1 - q * GROUP)
             mix_chunk(first, GROUP)
 
-    block = CHUNK * cols
-    wide = block + 2 * cols
-    lane = lax.broadcasted_iota(jnp.int32, (1, 256), 1)
-    line = jnp.zeros((1, 256), jnp.float32)
-    for k in range(filter_ref.shape[1]):
-        line = jnp.where(lane == k + cols - filter_ref.shape[1] // 2, filter_ref[0, k], line)
-    weights = pltpu.roll(jnp.broadcast_to(line, (block, 256)), 0, 1, stride=1, stride_axis=0)
-    weights = weights[:, :wide]
-    high = weights.astype(jnp.bfloat16)
-    rest = (weights - high.astype(jnp.float32)).astype(jnp.bfloat16)
-    place = mine * GROUP + middle * GROUP + 12
-
-    def block_at(i):
-        return pl.ds(pl.multiple_of(lax.rem(place + i * CHUNK, owners) * cols, block), block)
-
-    def filtered(window):
-        total = jnp.dot(high, window, preferred_element_type=jnp.float32)
-        total += jnp.dot(rest, window, preferred_element_type=jnp.float32)
-        return total.astype(jnp.bfloat16)
-
     blocks = owners // CHUNK
     pieces[:, span(GROUP + owners, 2)] = pieces[:, span(GROUP, 2)]
     mixed[:, span(owners + 9, 4)] = mixed[:, span(9, 4)]
 
-    @pl.loop(0, blocks - 4)
-    def _(i):
-        window = mixed[:, span(11 + i * CHUNK, CHUNK + 2)]
-        result = filtered(jnp.concatenate([window[s] for s in range(SLOTS)], axis=1))
-        for s in range(SLOTS):
-            polar_result[s, block_at(i)] = result[:, s * channels : (s + 1) * channels]
+    @pl.loop(0, 4)
+    def _(k):
+        filter_block(k + lax.div(k, 2) * 8)
 
     arrived(groups, GROUP)
     mix_chunk(owners - 1, GROUP + 2)

time: 44.6 us -> 44.4 us (level)
  no operation moved by 1% of the time
where the time goes in v7:
time: 44.4 us; the launch traced here: 43.7 us
  Pallas kernels  43.1 us (97%)
  between operations  0.64 us (1%)
    pallas_call x1, Pallas kernels, layer(): pl.pallas_call(layer_kernel, out_shape=(jax.ShapeDtypeStruct(field.shape,...  41.9 us
    pallas_call x1, Pallas kernels, write(): pl.pallas_call(write_kernel, out_shape=tuple((jax.ShapeDtypeStruct(x.shap...  1.19 us

profile of v7, /device:TPU:1, one launch (start us, length us, event | category | flops | bytes accessed | tf_op | source)
XLA Modules:
  0.0 43.7 jit_solution(14700979938290392011)
XLA Ops:
  0.6 41.9 %shard_map.104 = (bf16[64,32,128]{2,1,0:T(8,128)(2,1)S(1)}, bf16[2,2048,128]{2,1,0:T(8,128)(2,1)S(1)}) custom-call(s32[1,32]{1,0:T(1,128)} %bitcast.6, s32[1,32]{1,0:T(1,128)} %bitcast.7, f32[1,31]{1,0:T(1,128)} %bitcast.8, bf16[64,32,128]{2,1,0:T(8,128)(2,1)} %field_hbm.1, s32[32,64]{1,0:T(8,128)} %bitcast.5, f32[15,128]{1,0:T(8,128)} %taps_hbm.1, ...), custom_call_target="tpu_custom_call" | custom-call | tf_op jit(solution)/shard_map/pallas_call | solution.py:370
  42.5 1.2 %shard_map.105 = (bf16[64,32,128]{2,1,0:T(8,128)(2,1)}, bf16[2,2048,128]{2,1,0:T(8,128)(2,1)}) custom-call(bf16[64,32,128]{2,1,0:T(8,128)(2,1)S(1)} %get-tuple-element.4.field_ref, bf16[2,2048,128]{2,1,0:T(8,128)(2,1)S(1)} %get-tuple-element.5.polar_ref), custom_call_target="tpu_custom_call" | custom-call | tf_op jit(solution)/shard_map/pallas_call | solution.py:421
